TPU v7x, 32 devices: a whole 2x2x4 slice. The times are simulated.
32 devices in a mesh: row: 4 (over y, x), col: 8 (over z, core).
Axes of the slice: x: 2, y: 2, z: 4, core: 2. Of those that a mesh axis runs over, the one named last changes fastest.
Arguments:
- latent: bfloat16 [128, 256, 512], P('row', 'col'), may hold values from -12 to 12
- conv_scale: float32 [512], replicated, may hold values from 0.5 to 1.5
- conv_shift: float32 [512], replicated, may hold values from -3 to 3
- expand_weight: bfloat16 [512, 2048], replicated, may hold values from -0.25 to 0.25
- depth_kernel: float32 [9, 2048], replicated, may hold values from -2 to 2
- squeeze_down: bfloat16 [2048, 128], replicated, may hold values from -0.5 to 0.5
- squeeze_up: bfloat16 [128, 2048], replicated, may hold values from -0.5 to 0.5
- project_weight: bfloat16 [2048, 512], replicated, may hold values from -0.125 to 0.125
- block_gain: float32 [512], replicated, may hold values from 0.5 to 1.5
- block_projection: bfloat16 [512, 1536], replicated, may hold values from -0.25 to 0.25
- block_output: bfloat16 [512, 512], replicated, may hold values from -0.25 to 0.25
- block_table: float32 [16, 225], replicated, may hold values from -4 to 300
- first_gain: float32 [512], replicated, may hold values from 0.5 to 1.5
- first_expand: bfloat16 [512, 2048], replicated, may hold values from -0.25 to 0.25
- first_reduce: bfloat16 [2048, 512], replicated, may hold values from -0.125 to 0.125
- grid_gain: float32 [512], replicated, may hold values from 0.5 to 1.5
- grid_projection: bfloat16 [512, 1536], replicated, may hold values from -0.25 to 0.25
- grid_output: bfloat16 [512, 512], replicated, may hold values from -0.25 to 0.25
- grid_table: float32 [16, 225], replicated, may hold values from -4 to 300
- second_gain: float32 [512], replicated, may hold values from 0.5 to 1.5
- second_expand: bfloat16 [512, 2048], replicated, may hold values from -0.25 to 0.25
- second_reduce: bfloat16 [2048, 512], replicated, may hold values from -0.125 to 0.125
Outputs:
- nowcast_latent: bfloat16 [128, 256, 512], P('row', 'col')
All inputs are finite; a program needn't handle non-finite values.
Results may differ from a plain program's by a relative error of at most 0.012.
Values may be sent and summed in bfloat16 or wider, within the bound.
A program may use at most 128 MiB of HBM per device.

v0:
```python
import functools

import jax
import jax.numpy as jnp
import numpy as np
from jax import lax
from jax.experimental import pallas as pl
from jax.experimental.pallas import tpu as pltpu
from jax.sharding import PartitionSpec as P

WIN = 8


def extended(cells, sides, width):
    for axis, dim in sides:
        count = lax.axis_size(axis)
        ends = count - 1
        head = lax.slice_in_dim(cells, 0, width, axis=dim)
        tail = lax.slice_in_dim(cells, cells.shape[dim] - width, cells.shape[dim], axis=dim)
        cells = jnp.concatenate(
            [
                lax.ppermute(tail, axis, [(i, (i + 1) % count) for i in range(ends)]),
                cells,
                lax.ppermute(head, axis, [((i + 1) % count, i) for i in range(ends)]),
            ],
            axis=dim,
        )
    return cells


def layer_norm_apply(values, norm_gain):
    widened = values.astype(jnp.float32)
    center = widened - jnp.mean(widened, axis=-1, keepdims=True)
    spread = jnp.mean(center * center, axis=-1, keepdims=True)
    return (center * lax.rsqrt(spread + 1e-05) * norm_gain).astype(jnp.bfloat16)


def position_bias(offset_bias_lookup):
    spots = offset_bias_lookup.shape[1]
    position = jnp.arange(WIN * WIN)
    down_pos = position // WIN
    across = position % WIN
    relative = (down_pos[:, None] - down_pos[None, :] + WIN - 1) * (2 * WIN - 1) + (
        across[:, None] - across[None, :] + WIN - 1
    )
    indicator_matrix = (relative[:, :, None] == jnp.arange(spots)[None, None, :]).astype(
        jnp.float32
    )
    return jnp.einsum(
        "bp,rjp->brj", offset_bias_lookup, indicator_matrix, precision=lax.Precision.HIGHEST
    )


def attend(triple, pos_bias):
    window_count, tokens, three_width = triple.shape
    feature_width = three_width // 3
    head_count = pos_bias.shape[0]
    head_size = feature_width // head_count
    queries = triple[..., :feature_width].reshape(window_count, tokens, head_count, head_size)
    key_row_list = triple[..., feature_width : 2 * feature_width].reshape(
        window_count, tokens, head_count, head_size
    )
    values = triple[..., 2 * feature_width :].reshape(window_count, tokens, head_count, head_size)
    scores = (
        jnp.einsum("nqhd,nkhd->nhqk", queries, key_row_list, preferred_element_type=jnp.float32)
        * head_size ** (-0.5)
        + pos_bias[None]
    )
    row_max = jnp.max(scores, axis=-1, keepdims=True)
    weight_tensors = jnp.exp(scores - row_max)
    attention_weight_map = (
        weight_tensors / jnp.sum(weight_tensors, axis=-1, keepdims=True)
    ).astype(jnp.bfloat16)
    mixed = jnp.einsum(
        "nhqk,nkhd->nqhd", attention_weight_map, values, preferred_element_type=jnp.float32
    )
    return mixed.astype(jnp.bfloat16).reshape(window_count, tokens, feature_width)


def attention_sublayer(windows, norm_gain, in_weight, out_weight, pos_bias):
    normed = layer_norm_apply(windows, norm_gain)
    triple = jnp.dot(normed, in_weight, preferred_element_type=jnp.float32).astype(jnp.bfloat16)
    mixed = attend(triple, pos_bias)
    return (
        windows.astype(jnp.float32) + jnp.dot(mixed, out_weight, preferred_element_type=jnp.float32)
    ).astype(jnp.bfloat16)


def feed_forward(values, norm_gain, in_weight, out_weight):
    normed = layer_norm_apply(values, norm_gain)
    hidden = jax.nn.gelu(
        jnp.dot(normed, in_weight, preferred_element_type=jnp.float32), approximate=True
    ).astype(jnp.bfloat16)
    return (
        values.astype(jnp.float32) + jnp.dot(hidden, out_weight, preferred_element_type=jnp.float32)
    ).astype(jnp.bfloat16)


def to_blocks(field):
    row_count, col_count, feats = field.shape
    return (
        field.reshape(row_count // WIN, WIN, col_count // WIN, WIN, feats)
        .transpose(0, 2, 1, 3, 4)
        .reshape(-1, WIN * WIN, feats)
    )


def from_blocks(windows, row_count, col_count):
    feats = windows.shape[-1]
    return (
        windows.reshape(row_count // WIN, col_count // WIN, WIN, WIN, feats)
        .transpose(0, 2, 1, 3, 4)
        .reshape(row_count, col_count, feats)
    )


def axis_shape(length, devices):
    fold = max(1, WIN // devices)
    rest = length // max(devices, WIN)
    span = min(devices, WIN)
    return (fold, rest, span, devices // span)


def grid_layout(field):
    row_devices = lax.axis_size("row")
    col_devices = lax.axis_size("col")
    row_count, col_count, feats = field.shape
    row_fold, row_rest, row_span, row_hop = axis_shape(row_count, row_devices)
    col_fold, col_rest, col_span, col_hop = axis_shape(col_count, col_devices)
    ordered_layout = field.reshape(
        row_fold, row_devices, row_rest, col_fold, col_devices, col_rest, feats
    )
    flat = ordered_layout.transpose(1, 4, 0, 2, 3, 5, 6).reshape(
        row_devices * col_devices, row_fold, row_rest, col_fold, col_rest, feats
    )
    flat = lax.all_to_all(flat, ("row", "col"), split_axis=0, concat_axis=0, tiled=True)
    moved = flat.reshape(
        row_devices, col_devices, row_fold, row_rest, col_fold, col_rest, feats
    ).transpose(2, 0, 3, 4, 1, 5, 6)
    moved = moved.reshape(
        row_fold, row_span, row_hop, row_rest, col_fold, col_span, col_hop, col_rest, feats
    )
    return moved.transpose(2, 3, 6, 7, 1, 0, 5, 4, 8).reshape(-1, WIN * WIN, feats)


def spatial_layout(windows, row_count, col_count):
    row_devices = lax.axis_size("row")
    col_devices = lax.axis_size("col")
    feats = windows.shape[-1]
    row_fold, row_rest, row_span, row_hop = axis_shape(row_count, row_devices)
    col_fold, col_rest, col_span, col_hop = axis_shape(col_count, col_devices)
    gridded = windows.reshape(
        row_hop, row_rest, col_hop, col_rest, row_span, row_fold, col_span, col_fold, feats
    )
    ordered_layout = gridded.transpose(5, 4, 0, 1, 7, 6, 2, 3, 8).reshape(
        row_fold, row_devices, row_rest, col_fold, col_devices, col_rest, feats
    )
    flat = ordered_layout.transpose(1, 4, 0, 2, 3, 5, 6).reshape(
        row_devices * col_devices, row_fold, row_rest, col_fold, col_rest, feats
    )
    flat = lax.all_to_all(flat, ("row", "col"), split_axis=0, concat_axis=0, tiled=True)
    moved = flat.reshape(
        row_devices, col_devices, row_fold, row_rest, col_fold, col_rest, feats
    ).transpose(2, 0, 3, 4, 1, 5, 6)
    return moved.reshape(row_count, col_count, feats)


def squeeze_gate(pooled, squeeze_down, squeeze_up):
    reduced = jax.nn.silu(
        jnp.dot(pooled[None, :], squeeze_down.astype(jnp.float32), precision=lax.Precision.HIGHEST)
    )
    return jax.nn.sigmoid(
        jnp.dot(reduced, squeeze_up.astype(jnp.float32), precision=lax.Precision.HIGHEST)
    )[0]


def axis_sum_kernel(axis, count, x_ref, o_ref, slots, send_sem, recv_sem):
    me = lax.axis_index(axis)
    barrier = pltpu.get_barrier_semaphore()
    peers = [lax.rem(me + step, count) for step in range(1, count)]
    for peer in peers:
        pl.semaphore_signal(
            barrier, inc=1, device_id={axis: peer}, device_id_type=pl.DeviceIdType.MESH
        )
    pl.semaphore_wait(barrier, count - 1)
    copies = []
    for step, peer in enumerate(peers):
        copy = pltpu.make_async_remote_copy(
            src_ref=x_ref,
            dst_ref=slots.at[step],
            send_sem=send_sem.at[step],
            recv_sem=recv_sem.at[step],
            device_id={axis: peer},
            device_id_type=pl.DeviceIdType.MESH,
        )
        copy.start()
        copies.append(copy)
    for copy in copies:
        copy.wait()
    total = x_ref[...]
    for step in range(count - 1):
        total = total + slots[step]
    o_ref[...] = total


def axis_sum(values, axis, collective_id):
    count = lax.axis_size(axis)
    if count == 1:
        return values
    return pl.pallas_call(
        functools.partial(axis_sum_kernel, axis, count),
        out_shape=jax.ShapeDtypeStruct(values.shape, values.dtype),
        in_specs=[pl.BlockSpec(memory_space=pltpu.VMEM)],
        out_specs=pl.BlockSpec(memory_space=pltpu.VMEM),
        scratch_shapes=[
            pltpu.VMEM((count - 1,) + values.shape, values.dtype),
            pltpu.SemaphoreType.DMA((count - 1,)),
            pltpu.SemaphoreType.DMA((count - 1,)),
        ],
        compiler_params=pltpu.CompilerParams(
            collective_id=collective_id, has_side_effects=True, vmem_limit_bytes=4 * 1024 * 1024
        ),
        name="axis_sum_" + axis,
    )(values)


LANES = 128
GROUP = 256


def normed_rows(widened, gain):
    center = widened - jnp.mean(widened, axis=-1, keepdims=True)
    spread = jnp.mean(center * center, axis=-1, keepdims=True)
    return (center * lax.rsqrt(spread + 1e-05) * gain).astype(jnp.bfloat16)


def mixer_kernel(
    layout, head_size, x_ref, gain_ref, bias_ref, late_gain_ref, proj_hbm, out_hbm, up_hbm, down_hbm,
    o_ref, triple, heads, proj_ref, out_w_ref, up_ref, down_ref, sems,
):
    kind, across = layout
    rows_total, feats = x_ref.shape
    tokens = WIN * WIN
    window_count = rows_total // tokens
    slabs = feats // LANES
    per_slab = LANES // head_size
    moves = [
        pltpu.make_async_copy(src, dst, sems.at[k])
        for k, (src, dst) in enumerate(
            ((proj_hbm, proj_ref), (out_hbm, out_w_ref), (up_hbm, up_ref), (down_hbm, down_ref))
        )
    ]
    moves[0].start()
    moves[0].wait()
    for move in moves[1:]:
        move.start()
    chunk = 256

    def project(step, carry):
        rows = pl.ds(pl.multiple_of(step * chunk, chunk), chunk)
        normed = normed_rows(x_ref[rows, :].astype(jnp.float32), gain_ref[...])
        for part in range(3 * slabs // 2):
            product = jnp.dot(
                normed, proj_ref[:, part * GROUP : (part + 1) * GROUP],
                preferred_element_type=jnp.float32,
            ).astype(jnp.bfloat16).astype(jnp.float32)
            triple[2 * part, rows, :] = product[:, :LANES]
            triple[2 * part + 1, rows, :] = product[:, LANES:]
        return carry

    lax.fori_loop(0, rows_total // chunk, project, 0)

    def places(window):
        if kind == "strided":
            return [pl.ds(window, tokens, stride=across)]
        per_row = across // WIN
        base = (window // per_row) * (WIN * across) + (window % per_row) * WIN
        return [pl.ds(pl.multiple_of(base + r * across, WIN), WIN) for r in range(WIN)]

    lane = lax.broadcasted_iota(jnp.int32, (tokens, GROUP), 1)
    head_of = (lane % LANES) // head_size
    scale = head_size ** (-0.5)

    def one_window(window):
        spots = places(window)

        def fetch(slab):
            pieces = [triple[slab, spot, :] for spot in spots]
            whole = pieces[0] if len(pieces) == 1 else jnp.concatenate(pieces, axis=0)
            return whole

        empty = jnp.zeros((tokens, LANES), jnp.bfloat16)
        for group in range(slabs // 2):
            first, second = 2 * group, 2 * group + 1
            query_0 = fetch(first).astype(jnp.bfloat16)
            query_1 = fetch(second).astype(jnp.bfloat16)
            keys = jnp.concatenate([fetch(slabs + first), fetch(slabs + second)], axis=1)
            vals = jnp.concatenate([fetch(2 * slabs + first), fetch(2 * slabs + second)], axis=1)
            block_q = jnp.concatenate(
                [
                    jnp.concatenate([query_0, empty], axis=1),
                    jnp.concatenate([empty, query_1], axis=1),
                ],
                axis=0,
            )
            block_k = jnp.concatenate(
                [jnp.where(head_of == j, keys, 0.0).astype(jnp.bfloat16) for j in range(per_slab)],
                axis=0,
            )
            block_v = jnp.concatenate(
                [jnp.where(head_of == j, vals, 0.0).astype(jnp.bfloat16) for j in range(per_slab)],
                axis=0,
            )
            scores = lax.dot_general(
                block_k, block_q, (((1,), (1,)), ((), ())), preferred_element_type=jnp.float32
            )
            scores = (scores * scale + bias_ref[group]).reshape(per_slab, tokens, 2 * tokens)
            weights = jnp.exp(scores - jnp.max(scores, axis=1, keepdims=True))
            shares = weights * (1.0 / jnp.sum(weights, axis=1, keepdims=True))
            shares = shares.reshape(per_slab * tokens, 2 * tokens).astype(jnp.bfloat16)
            mixed = lax.dot_general(
                shares, block_v, (((0,), (0,)), ((), ())), preferred_element_type=jnp.float32
            )
            for slab, part in (
                (first, mixed[:tokens, :LANES]), (second, mixed[tokens:, LANES:])
            ):
                if len(spots) == 1:
                    heads[slab, spots[0], :] = part
                else:
                    for r, spot in enumerate(spots):
                        heads[slab, spot, :] = part[r * WIN : (r + 1) * WIN]

    def attend_pair(step, carry):
        one_window(2 * step)
        one_window(2 * step + 1)
        return carry

    lax.fori_loop(0, window_count // 2, attend_pair, 0)
    for move in moves[1:]:
        move.wait()
    hidden_width = up_ref.shape[1]
    tile = 512

    def feed(step, carry):
        rows = pl.ds(pl.multiple_of(step * chunk, chunk), chunk)
        mixed = jnp.concatenate([heads[s, rows, :] for s in range(slabs)], axis=1).astype(jnp.bfloat16)
        value = (
            x_ref[rows, :].astype(jnp.float32)
            + jnp.dot(mixed, out_w_ref[...], preferred_element_type=jnp.float32)
        ).astype(jnp.bfloat16).astype(jnp.float32)
        normed = normed_rows(value, late_gain_ref[...])
        for k in range(hidden_width // tile):
            part = slice(k * tile, (k + 1) * tile)
            hidden = jax.nn.gelu(
                jnp.dot(normed, up_ref[:, part], preferred_element_type=jnp.float32),
                approximate=True,
            ).astype(jnp.bfloat16)
            value = value + jnp.dot(hidden, down_ref[part, :], preferred_element_type=jnp.float32)
        o_ref[rows, :] = value.astype(jnp.bfloat16)
        return carry

    lax.fori_loop(0, rows_total // chunk, feed, 0)


def mixer(x, layout, gain, in_weight, out_weight, bias, late_gain, up, down, heads_count):
    rows, feats = x.shape
    vmem = pl.BlockSpec(memory_space=pltpu.VMEM)
    hbm = pl.BlockSpec(memory_space=pltpu.HBM)
    flops = 8 * rows * feats * (4 * feats + 2 * up.shape[1])
    return pl.pallas_call(
        functools.partial(mixer_kernel, layout, feats // heads_count),
        out_shape=jax.ShapeDtypeStruct((rows, feats), jnp.bfloat16),
        in_specs=[vmem] * 4 + [hbm] * 4,
        out_specs=vmem,
        scratch_shapes=[
            pltpu.VMEM((3 * feats // LANES, rows, LANES), jnp.float32),
            pltpu.VMEM((feats // LANES, rows, LANES), jnp.float32),
            pltpu.VMEM(in_weight.shape, jnp.bfloat16),
            pltpu.VMEM(out_weight.shape, jnp.bfloat16),
            pltpu.VMEM(up.shape, jnp.bfloat16),
            pltpu.VMEM(down.shape, jnp.bfloat16),
            pltpu.SemaphoreType.DMA((4,)),
        ],
        compiler_params=pltpu.CompilerParams(vmem_limit_bytes=60 * 1024 * 1024),
        cost_estimate=pl.CostEstimate(
            flops=flops, bytes_accessed=12 * 1024 * 1024, transcendentals=0
        ),
        name="mixer_" + layout[0],
    )(x, gain[None], bias, late_gain[None], in_weight, out_weight, up, down)


def key_major_bias(table, down, across):
    head_count, spots = table.shape
    relative = (down[None, :] - down[:, None] + WIN - 1) * (2 * WIN - 1) + (
        across[None, :] - across[:, None] + WIN - 1
    )
    tokens = WIN * WIN
    chosen = (jnp.arange(spots)[:, None] == jnp.asarray(relative.reshape(-1))[None, :]).astype(
        jnp.float32
    )
    spread = jnp.dot(table, chosen, precision=lax.Precision.HIGHEST)
    return (
        spread.reshape(head_count // 8, 2, 4, tokens, tokens)
        .transpose(0, 2, 3, 1, 4)
        .reshape(head_count // 8, 4 * tokens, 2 * tokens)
    )


def split_sublayers(conv_out, run_block, run_grid, block_table, grid_table):
    row_devices = lax.axis_size("row")
    col_devices = lax.axis_size("col")
    row_count, col_count, feats = conv_out.shape
    plain = np.arange(WIN * WIN)
    block_bias = key_major_bias(block_table, plain // WIN, plain % WIN)
    if row_devices > WIN or col_devices > WIN:
        section = run_block(conv_out.reshape(-1, feats), ("blocks", col_count), block_bias)
        windows = grid_layout(section.reshape(row_count, col_count, feats))
        count = windows.shape[0]
        bias = key_major_bias(grid_table, plain // WIN, plain % WIN)
        out = run_grid(windows.transpose(1, 0, 2).reshape(-1, feats), ("strided", count), bias)
        out = out.reshape(WIN * WIN, count, feats).transpose(1, 0, 2)
        return spatial_layout(out, row_count, col_count)
    devices = row_devices * col_devices
    row_fold, col_fold = WIN // row_devices, WIN // col_devices
    row_rest, col_rest = row_count // row_fold, col_count // col_fold
    parts = row_rest // WIN
    count = WIN * col_rest // devices
    pieces = col_rest // count
    order = np.arange(WIN * WIN).reshape(row_devices, col_devices, row_fold, col_fold)
    at = np.indices(order.shape).reshape(4, -1)
    grid_bias = key_major_bias(grid_table, at[0] * row_fold + at[2], at[1] * col_fold + at[3])
    strips = conv_out.reshape(row_fold, parts, WIN, col_count, feats)
    results = []
    for part in range(parts):
        section = run_block(
            strips[:, part].reshape(-1, feats), ("blocks", col_count), block_bias
        )
        sent = (
            section.reshape(row_fold, WIN, col_fold, pieces, count, feats)
            .transpose(1, 3, 0, 2, 4, 5)
            .reshape(devices, row_fold * col_fold * count, feats)
        )
        got = lax.all_to_all(sent, ("row", "col"), split_axis=0, concat_axis=0, tiled=True)
        out = run_grid(got.reshape(-1, feats), ("strided", count), grid_bias)
        back = lax.all_to_all(
            out.reshape(devices, -1, feats), ("row", "col"), split_axis=0, concat_axis=0, tiled=True
        )
        results.append(
            back.reshape(WIN, pieces, row_fold, col_fold, count, feats)
            .transpose(2, 0, 3, 1, 4, 5)
            .reshape(row_fold, WIN, col_count, feats)
        )
    return jnp.stack(results, axis=1).reshape(row_count, col_count, feats)


PAD = 8


def conv_kernel(
    row_count, col_count, flags, ext_ref, scale_ref, shift_ref, expand_ref, taps_ref,
    o_ref, sums_ref, conv_in, expanded,
):
    wide = col_count + PAD
    tall = row_count + 2
    width = expand_ref.shape[1]
    block = expanded.shape[-1]
    bounds = [8 * k for k in range(row_count // 8)] + [tall]
    for low, high in zip(bounds[:-1], bounds[1:]):
        rows = slice(low * wide, high * wide)
        conv_in[rows, :] = (
            ext_ref[rows, :].astype(jnp.float32) * scale_ref[...] + shift_ref[...]
        ).astype(jnp.bfloat16)
    spot = lax.broadcasted_iota(jnp.int32, (1, PAD, block), 1)
    side = jnp.where(spot == 0, flags[3], jnp.where(spot == PAD - 1, flags[2], 0.0))

    def channels(step, carry):
        lanes = pl.ds(pl.multiple_of(step * block, block), block)
        for low, high in zip(bounds[:-1], bounds[1:]):
            product = jnp.dot(
                conv_in[low * wide : high * wide, :], expand_ref[:, lanes],
                preferred_element_type=jnp.float32,
            )
            value = jax.nn.gelu(product, approximate=True).astype(jnp.bfloat16)
            expanded[low:high] = value.astype(jnp.float32).reshape(high - low, wide, block)
        expanded[0] = expanded[0] * flags[0]
        expanded[tall - 1] = expanded[tall - 1] * flags[1]
        expanded[:, col_count:, :] = expanded[:, col_count:, :] * side
        for half in range(block // LANES):
            inner = slice(half * LANES, (half + 1) * LANES)
            outer = pl.ds(pl.multiple_of(step * block + half * LANES, LANES), LANES)
            taps = [taps_ref[k : k + 1, outer] for k in range(9)]

            def rows_of(group, total):
                base = group * 4
                held = [expanded[base + k, :, inner] for k in range(6)]
                for k in range(4):
                    parts = [
                        held[k] * taps[side_step]
                        + held[k + 1] * taps[3 + side_step]
                        + held[k + 2] * taps[6 + side_step]
                        for side_step in range(3)
                    ]
                    summed = (
                        pltpu.roll(parts[0], 1, 0) + parts[1] + pltpu.roll(parts[2], wide - 1, 0)
                    )[:col_count]
                    deep = jax.nn.gelu(summed, approximate=True)
                    total = total + jnp.sum(deep.reshape(col_count // 8, 8, LANES), axis=0)
                    at = pl.ds(pl.multiple_of((base + k) * col_count, col_count), col_count)
                    o_ref[at, outer] = deep.astype(o_ref.dtype)
                return total

            total = lax.fori_loop(0, row_count // 4, rows_of, jnp.zeros((8, LANES), jnp.float32))
            sums_ref[:, outer] = jnp.sum(total, axis=0, keepdims=True)
        return carry

    lax.fori_loop(0, width // block, channels, 0)


def depthwise_stage(latent, conv_scale, conv_shift, expand_weight, depth_kernel):
    row_count, col_count, feats = latent.shape
    width = expand_weight.shape[1]
    row_at, col_at = lax.axis_index("row"), lax.axis_index("col")
    flags = jnp.stack(
        [row_at > 0, row_at < lax.axis_size("row") - 1, col_at > 0, col_at < lax.axis_size("col") - 1]
    ).astype(jnp.float32)
    tall = extended(latent, (("row", 0),), 1)
    count = lax.axis_size("col")
    ahead = [(i, i + 1) for i in range(count - 1)]
    left = lax.ppermute(tall[:, col_count - 1 :], "col", ahead)
    right = lax.ppermute(tall[:, :1], "col", [(b, a) for a, b in ahead])
    blank = jnp.zeros((row_count + 2, PAD - 2, feats), latent.dtype)
    ext = jnp.concatenate([tall, right, blank, left], axis=1).reshape(-1, feats)
    vmem = pl.BlockSpec(memory_space=pltpu.VMEM)
    block = 256
    return pl.pallas_call(
        functools.partial(conv_kernel, row_count, col_count),
        out_shape=(
            jax.ShapeDtypeStruct((row_count * col_count, width), jnp.bfloat16),
            jax.ShapeDtypeStruct((1, width), jnp.float32),
        ),
        in_specs=[pl.BlockSpec(memory_space=pltpu.SMEM)] + [vmem] * 5,
        out_specs=(vmem, vmem),
        scratch_shapes=[
            pltpu.VMEM(ext.shape, jnp.bfloat16),
            pltpu.VMEM((row_count + 2, col_count + PAD, block), jnp.float32),
        ],
        compiler_params=pltpu.CompilerParams(vmem_limit_bytes=20 * 1024 * 1024),
        name="conv_stage",
    )(flags, ext, conv_scale[None], conv_shift[None], expand_weight, depth_kernel)


def per_device(
    latent,
    conv_scale,
    conv_shift,
    expand_weight,
    depth_kernel,
    squeeze_down,
    squeeze_up,
    project_weight,
    block_gain,
    block_projection,
    block_output,
    block_table,
    first_gain,
    first_expand,
    first_reduce,
    grid_gain,
    grid_projection,
    grid_output,
    grid_table,
    second_gain,
    second_expand,
    second_reduce,
):
    row_devices = lax.axis_size("row")
    col_devices = lax.axis_size("col")
    row_count, col_count, channels = latent.shape
    depthwise, local_sums = depthwise_stage(
        latent, conv_scale, conv_shift, expand_weight, depth_kernel
    )
    local_sums = local_sums.reshape(-1, LANES)
    channel_sums = axis_sum(axis_sum(local_sums, "row", 1), "col", 2).reshape(-1)
    pooled = channel_sums / (row_count * row_devices * col_count * col_devices)
    excite = squeeze_gate(pooled, squeeze_down, squeeze_up)
    gated = (depthwise.astype(jnp.float32) * excite).astype(jnp.bfloat16)
    conv_out = (
        latent.reshape(-1, channels).astype(jnp.float32)
        + jnp.dot(gated, project_weight, preferred_element_type=jnp.float32)
    ).astype(jnp.bfloat16).reshape(row_count, col_count, channels)

    def run_block(cells, layout, bias):
        return mixer(
            cells, layout, block_gain, block_projection, block_output, bias, first_gain,
            first_expand, first_reduce, block_table.shape[0],
        )

    def run_grid(cells, layout, bias):
        return mixer(
            cells, layout, grid_gain, grid_projection, grid_output, bias, second_gain,
            second_expand, second_reduce, grid_table.shape[0],
        )

    return split_sublayers(conv_out, run_block, run_grid, block_table, grid_table)


def solution(mesh):
    placed = (
        P("row", "col", None),
        P(),
        P(),
        P(),
        P(),
        P(),
        P(),
        P(),
        P(),
        P(),
        P(),
        P(),
        P(),
        P(),
        P(),
        P(),
        P(),
        P(),
        P(),
        P(),
        P(),
        P(),
    )
    return jax.shard_map(
        per_device, mesh=mesh, in_specs=placed, out_specs=P("row", "col", None), check_vma=False
    )
```

profile of v0, /device:TPU:5, one launch (start us, length us, event | category | flops | bytes accessed | tf_op | source)
XLA Modules:
  0.0 163.3 jit_solution(9568147631204398551)
XLA Ops:
  0.0 0.9 fusion.13
  0.9 3.2 %collective-permute-start = (bf16[1,32,512]{2,1,0:T(8,128)(2,1)S(1)}, bf16[1,32,512]{2,1,0:T(8,128)(2,1)S(1)}, u32[]{:S(2)}, u32[]{:S(2)}) collective-permute-start(bf16[1,32,512]{2,1,0:T(8,128)(2,1)S(1)} %get-tuple-element.14), channel_id=1, source_target_pairs={{0,8},{8,16},{16,24},{1,9},{9,17},{17,25},{2,10},{10,18},{18,26},{... | collective-permute-start | bytes 98312 | tf_op jit(solution)/shard_map/ppermute | solution.py:22
  4.2 3.1 %collective-permute-start.1 = (bf16[1,32,512]{2,1,0:T(8,128)(2,1)S(1)}, bf16[1,32,512]{2,1,0:T(8,128)(2,1)S(1)}, u32[]{:S(2)}, u32[]{:S(2)}) collective-permute-start(bf16[1,32,512]{2,1,0:T(8,128)(2,1)S(1)} %get-tuple-element.13), channel_id=1, source_target_pairs={{8,0},{16,8},{24,16},{9,1},{17,9},{25,17},{10,2},{18,10},{26,18},{... | collective-permute-start | bytes 98312 | tf_op jit(solution)/shard_map/ppermute | solution.py:24
  7.3 2.8 %convolution_bitcast_fusion.1 = f32[16,4096]{1,0:T(8,128)} fusion(f32[16,225]{1,0:T(8,128)} %param.35, s32[4096]{0:T(1024)} %constant.27.clone), kind=kOutput, calls=%fused_computation.2 | convolution fusion | flops 177868800 | bytes 292928 | tf_op jit(solution)/shard_map/dot_general | solution.py:401
  10.0 2.1 %convolution_bitcast_fusion = f32[16,4096]{1,0:T(8,128)S(1)} fusion(f32[16,225]{1,0:T(8,128)} %param.42, s32[4096]{0:T(1024)} %constant.28.clone), kind=kOutput, calls=%fused_computation.1 | convolution fusion | flops 177868800 | bytes 292928 | tf_op jit(solution)/shard_map/dot_general | solution.py:401
  12.3 0.9 fusion.11
  13.2 3.1 %collective-permute-start.2 = (bf16[34,1,512]{2,1,0:T(2,128)(2,1)}, bf16[34,1,512]{2,1,0:T(2,128)(2,1)}, u32[]{:S(2)}, u32[]{:S(2)}) collective-permute-start(bf16[34,1,512]{2,1,0:T(2,128)(2,1)} %get-tuple-element.9), channel_id=1, source_target_pairs={{1,0},{2,1},{3,2},{4,3},{5,4},{6,5},{7,6},{9,8},{10,9},{11,10},{12... | collective-permute-start | bytes 104456 | tf_op jit(solution)/shard_map/ppermute | solution.py:530
  16.3 3.3 %collective-permute-start.3 = (bf16[34,1,512]{2,1,0:T(2,128)(2,1)}, bf16[34,1,512]{2,1,0:T(2,128)(2,1)}, u32[]{:S(2)}, u32[]{:S(2)}) collective-permute-start(bf16[34,1,512]{2,1,0:T(2,128)(2,1)} %get-tuple-element.10), channel_id=1, source_target_pairs={{0,1},{1,2},{2,3},{3,4},{4,5},{5,6},{6,7},{8,9},{9,10},{10,11},{11... | collective-permute-start | bytes 104456 | tf_op jit(solution)/shard_map/ppermute | solution.py:529
  19.7 1.1 reshape.78
  20.8 0.4 copy.42
  21.3 1.0 reshape.79.bias_ref
  22.5 0.4 copy.41
  22.9 1.0 reshape.84.bias_ref
  24.1 2.1 %pad_maximum_fusion = bf16[34,40,512]{2,1,0:T(8,128)(2,1)S(1)} fusion(bf16[34,1,512]{2,1,0:T(2,128)(2,1)} %collective-permute-done.3, bf16[34,1,512]{2,1,0:T(2,128)(2,1)} %collective-permute-done.2, bf16[34,32,512]{2,1,0:T(8,128)(2,1)} %copy-done.5, bf16[40]{0:T(256)(128)(2,1)S(1)} %pad.4.clone), kind=kLoop, calls=%fused_computation.11 | loop fusion | flops 5570560 | bytes 2576464 | tf_op jit(solution)/shard_map/concatenate | solution.py:532
  26.2 18.9 %conv_stage.1 = (bf16[1024,2048]{1,0:T(8,128)(2,1)S(1)}, f32[1,2048]{1,0:T(1,128)S(1)}) custom-call(f32[4]{0:T(128)S(1)} %add_convert_fusion.flags, bf16[1360,512]{1,0:T(8,128)(2,1)S(1)} %bitcast.71, f32[1,512]{1,0:T(1,128)S(1)} %bitcast.73, f32[1,512]{1,0:T(1,128)S(1)} %bitcast.74, bf16[512,2048]{1,0:T(8,128)(2,1)S(1)} %copy-done.1, f32[9,2048]{1,0:T(8,128)S(1)} %copy-done.2), custom_call_target="tpu_custom_call" | custom-call | tf_op jit(solution)/shard_map/conv_stage/pallas_call | solution.py:535
  45.1 3.5 %axis_sum_row.1.x_ref = f32[16,128]{1,0:T(8,128)S(1)} custom-call(f32[16,128]{1,0:T(8,128)S(1)} %bitcast.72), custom_call_target="tpu_custom_call" | custom-call | tf_op jit(solution)/shard_map/axis_sum_row/pallas_call | solution.py:210
  48.6 6.9 %axis_sum_col.1 = f32[16,128]{1,0:T(8,128)S(1)} custom-call(f32[16,128]{1,0:T(8,128)S(1)} %axis_sum_row.1.x_ref), custom_call_target="tpu_custom_call" | custom-call | tf_op jit(solution)/shard_map/axis_sum_col/pallas_call | solution.py:210
  56.2 2.3 %fusion.2 = bf16[1024,512]{1,0:T(8,128)(2,1)S(1)} fusion(bf16[1024,512]{1,0:T(8,128)(2,1)S(1)} %bitcast.81, bf16[2048,512]{1,0:T(8,128)(2,1)S(1)} %copy-done, bf16[1024,2048]{1,0:T(8,128)(2,1)S(1)} %get-tuple-element.7, f32[2048]{0:T(1024)S(1)} %add_divide_fusion), kind=kOutput, calls=%fused_computation.8 | convolution fusion | flops 2155347968 | bytes 8396800 | tf_op jit(solution)/shard_map/dot_general | solution.py:589
  58.5 1.1 fusion.12
  59.6 14.9 %mixer_blocks.3 = bf16[512,512]{1,0:T(8,128)(2,1)} custom-call(bf16[512,512]{1,0:T(8,128)(2,1)} %bitcast.90, f32[1,512]{1,0:T(1,128)} %bitcast.93, f32[2,256,128]{2,1,0:T(8,128)} %reshape.79.bias_ref, f32[1,512]{1,0:T(1,128)} %bitcast.95, bf16[512,1536]{1,0:T(8,128)(2,1)} %proj_hbm.6, bf16[512,512]{1,0:T(8,128)(2,1)} %out_hbm.6, bf16[512,2048]{1,0:T(8,128)(2,1)} %up_hbm.6, ...), custom_call_target="tpu_custom_call" | custom-call | flops 12884901888 | bytes 12582912 | tf_op jit(solution)/shard_map/mixer_blocks/pallas_call | solution.py:370
  74.5 1.9 %copy.31 = bf16[8,4,2,1,8,512]{5,4,2,1,0,3:T(8,128)(2,1)} copy(bf16[8,4,2,1,8,512]{5,4,1,0,2,3:T(8,128)(2,1)} %bitcast.88) | data formatting | bytes 1048576 | tf_op jit(solution)/shard_map/transpose | solution.py:440
  76.4 5.1 %all-to-all-start.2 = ((bf16[32,16,512]{2,1,0:T(8,128)(2,1)}), bf16[32,16,512]{2,1,0:T(8,128)(2,1)S(1)}, u32[]{:S(2)}, u32[]{:S(2)}) async-start(bf16[32,16,512]{2,1,0:T(8,128)(2,1)} %bitcast.35), calls=%async_computation.2 | async-start | bytes 1048576 | tf_op jit(solution)/shard_map/all_to_all | solution.py:443
  81.5 14.9 %mixer_blocks.2 = bf16[512,512]{1,0:T(8,128)(2,1)} custom-call(bf16[512,512]{1,0:T(8,128)(2,1)} %bitcast.89, f32[1,512]{1,0:T(1,128)} %bitcast.94, f32[2,256,128]{2,1,0:T(8,128)} %reshape.79.bias_ref, f32[1,512]{1,0:T(1,128)} %bitcast.96, bf16[512,1536]{1,0:T(8,128)(2,1)} %proj_hbm.6, bf16[512,512]{1,0:T(8,128)(2,1)} %out_hbm.6, bf16[512,2048]{1,0:T(8,128)(2,1)} %up_hbm.6, ...), custom_call_target="tpu_custom_call" | custom-call | flops 12884901888 | bytes 12582912 | tf_op jit(solution)/shard_map/mixer_blocks/pallas_call | solution.py:370
  96.4 1.9 %copy.27 = bf16[8,4,2,1,8,512]{5,4,2,1,0,3:T(8,128)(2,1)} copy(bf16[8,4,2,1,8,512]{5,4,1,0,2,3:T(8,128)(2,1)} %bitcast.87) | data formatting | bytes 1048576 | tf_op jit(solution)/shard_map/transpose | solution.py:440
  98.4 5.8 %all-to-all-start = ((bf16[32,16,512]{2,1,0:T(8,128)(2,1)}), bf16[32,16,512]{2,1,0:T(8,128)(2,1)S(1)}, u32[]{:S(2)}, u32[]{:S(2)}) async-start(bf16[32,16,512]{2,1,0:T(8,128)(2,1)} %bitcast.22), calls=%async_computation | async-start | bytes 1048576 | tf_op jit(solution)/shard_map/all_to_all | solution.py:443
  104.2 14.9 %mixer_strided.3 = bf16[512,512]{1,0:T(8,128)(2,1)} custom-call(bf16[512,512]{1,0:T(8,128)(2,1)} %bitcast.83, f32[1,512]{1,0:T(1,128)} %bitcast.97, f32[2,256,128]{2,1,0:T(8,128)} %reshape.84.bias_ref, f32[1,512]{1,0:T(1,128)} %bitcast.99, bf16[512,1536]{1,0:T(8,128)(2,1)} %proj_hbm.7, bf16[512,512]{1,0:T(8,128)(2,1)} %out_hbm.7, bf16[512,2048]{1,0:T(8,128)(2,1)} %up_hbm.7, ...), custom_call_target="tpu_custom_call" | custom-call | flops 12884901888 | bytes 12582912 | tf_op jit(solution)/shard_map/mixer_strided/pallas_call | solution.py:370
  119.5 5.5 %all-to-all-start.3 = ((bf16[32,16,512]{2,1,0:T(8,128)(2,1)}), bf16[32,16,512]{2,1,0:T(8,128)(2,1)S(1)}, u32[]{:S(2)}, u32[]{:S(2)}) async-start(bf16[32,16,512]{2,1,0:T(8,128)(2,1)} %bitcast.85), calls=%async_computation.3 | async-start | bytes 1048576 | tf_op jit(solution)/shard_map/all_to_all | solution.py:445
  125.0 14.9 %mixer_strided.2 = bf16[512,512]{1,0:T(8,128)(2,1)} custom-call(bf16[512,512]{1,0:T(8,128)(2,1)} %bitcast.84, f32[1,512]{1,0:T(1,128)} %bitcast.98, f32[2,256,128]{2,1,0:T(8,128)} %reshape.84.bias_ref, f32[1,512]{1,0:T(1,128)} %bitcast.100, bf16[512,1536]{1,0:T(8,128)(2,1)} %proj_hbm.7, bf16[512,512]{1,0:T(8,128)(2,1)} %out_hbm.7, bf16[512,2048]{1,0:T(8,128)(2,1)} %up_hbm.7, ...), custom_call_target="tpu_custom_call" | custom-call | flops 12884901888 | bytes 12582912 | tf_op jit(solution)/shard_map/mixer_strided/pallas_call | solution.py:370
  140.3 5.5 %all-to-all-start.1 = ((bf16[32,16,512]{2,1,0:T(8,128)(2,1)}), bf16[32,16,512]{2,1,0:T(8,128)(2,1)S(1)}, u32[]{:S(2)}, u32[]{:S(2)}) async-start(bf16[32,16,512]{2,1,0:T(8,128)(2,1)} %bitcast.86), calls=%async_computation.1 | async-start | bytes 1048576 | tf_op jit(solution)/shard_map/all_to_all | solution.py:445
  145.8 0.9 copy.39
  146.7 14.4 %all-to-all-done.1 = bf16[32,16,512]{2,1,0:T(8,128)(2,1)S(1)} async-done(((bf16[32,16,512]{2,1,0:T(8,128)(2,1)}), bf16[32,16,512]{2,1,0:T(8,128)(2,1)S(1)}, u32[]{:S(2)}, u32[]{:S(2)}) %all-to-all-start.1) | async-done | bytes 524320 | tf_op jit(solution)/shard_map/all_to_all | solution.py:445
  161.2 2.1 %pad_maximum_fusion.1 = bf16[2,2,8,32,512]{4,3,2,1,0:T(8,128)(2,1)} fusion(bf16[2,1,8,32,512]{4,3,2,1,0:T(8,128)(2,1)} %bitcast.79, bf16[2,1,8,32,512]{4,3,2,1,0:T(8,128)(2,1)S(1)} %bitcast.80), kind=kLoop, calls=%fused_computation.13 | loop fusion | flops 524288 | bytes 2097152 | tf_op jit(solution)/shard_map/stack | solution.py:453
  (43 shorter events, 2.0 us)
Async XLA Ops:
  0.0 56.2 %copy-start = (bf16[2048,512]{1,0:T(8,128)(2,1)S(1)}, bf16[2048,512]{1,0:T(8,128)(2,1)}, u32[]{:S(2)}) copy-start(bf16[2048,512]{1,0:T(8,128)(2,1)} %param.31) | copy-start | bytes 6291460
  0.0 12.1 %copy-start.6 = (bf16[32,32,512]{2,1,0:T(8,128)(2,1)S(1)}, bf16[32,32,512]{2,1,0:T(8,128)(2,1)}, u32[]{:S(2)}) copy-start(bf16[32,32,512]{2,1,0:T(8,128)(2,1)} %param.24) | copy-start | bytes 3145732
  0.9 11.2 %collective-permute-start = (bf16[1,32,512]{2,1,0:T(8,128)(2,1)S(1)}, bf16[1,32,512]{2,1,0:T(8,128)(2,1)S(1)}, u32[]{:S(2)}, u32[]{:S(2)}) collective-permute-start(bf16[1,32,512]{2,1,0:T(8,128)(2,1)S(1)} %get-tuple-element.14), channel_id=1, source_target_pairs={{0,8},{8,16},{16,24},{1,9},{9,17},{17,25},{2,10},{10,18},{18,26},{... | collective-permute-start | bytes 98312 | tf_op jit(solution)/shard_map/ppermute | solution.py:22
  4.2 8.0 %collective-permute-start.1 = (bf16[1,32,512]{2,1,0:T(8,128)(2,1)S(1)}, bf16[1,32,512]{2,1,0:T(8,128)(2,1)S(1)}, u32[]{:S(2)}, u32[]{:S(2)}) collective-permute-start(bf16[1,32,512]{2,1,0:T(8,128)(2,1)S(1)} %get-tuple-element.13), channel_id=1, source_target_pairs={{8,0},{16,8},{24,16},{9,1},{17,9},{25,17},{10,2},{18,10},{26,18},{... | collective-permute-start | bytes 98312 | tf_op jit(solution)/shard_map/ppermute | solution.py:24
  12.2 7.4 %copy-start.5 = (bf16[34,32,512]{2,1,0:T(8,128)(2,1)}, bf16[34,32,512]{2,1,0:T(8,128)(2,1)S(1)}, u32[]{:S(2)}) copy-start(bf16[34,32,512]{2,1,0:T(8,128)(2,1)S(1)} %constant_dynamic-update-slice_fusion) | copy-start | bytes 3342340
  13.2 10.9 %collective-permute-start.2 = (bf16[34,1,512]{2,1,0:T(2,128)(2,1)}, bf16[34,1,512]{2,1,0:T(2,128)(2,1)}, u32[]{:S(2)}, u32[]{:S(2)}) collective-permute-start(bf16[34,1,512]{2,1,0:T(2,128)(2,1)} %get-tuple-element.9), channel_id=1, source_target_pairs={{1,0},{2,1},{3,2},{4,3},{5,4},{6,5},{7,6},{9,8},{10,9},{11,10},{12... | collective-permute-start | bytes 104456 | tf_op jit(solution)/shard_map/ppermute | solution.py:530
  16.3 7.8 %collective-permute-start.3 = (bf16[34,1,512]{2,1,0:T(2,128)(2,1)}, bf16[34,1,512]{2,1,0:T(2,128)(2,1)}, u32[]{:S(2)}, u32[]{:S(2)}) collective-permute-start(bf16[34,1,512]{2,1,0:T(2,128)(2,1)} %get-tuple-element.10), channel_id=1, source_target_pairs={{0,1},{1,2},{2,3},{3,4},{4,5},{5,6},{6,7},{8,9},{9,10},{10,11},{11... | collective-permute-start | bytes 104456 | tf_op jit(solution)/shard_map/ppermute | solution.py:529
  22.5 3.7 %copy-start.2 = (f32[9,2048]{1,0:T(8,128)S(1)}, f32[9,2048]{1,0:T(8,128)}, u32[]{:S(2)}) copy-start(f32[9,2048]{1,0:T(8,128)} %taps_ref.1) | copy-start | bytes 221188
  22.5 3.7 %copy-start.3 = (f32[512]{0:T(512)S(1)}, f32[512]{0:T(512)}, u32[]{:S(2)}) copy-start(f32[512]{0:T(512)} %param.25) | copy-start | bytes 6148
  22.5 3.7 %copy-start.4 = (f32[512]{0:T(512)S(1)}, f32[512]{0:T(512)}, u32[]{:S(2)}) copy-start(f32[512]{0:T(512)} %param.26) | copy-start | bytes 6148
  24.0 2.2 %copy-start.1 = (bf16[512,2048]{1,0:T(8,128)(2,1)S(1)}, bf16[512,2048]{1,0:T(8,128)(2,1)}, u32[]{:S(2)}) copy-start(bf16[512,2048]{1,0:T(8,128)(2,1)} %expand_ref.1) | copy-start | bytes 6291460
  26.1 29.3 %copy-start.8 = (bf16[2048,128]{1,0:T(8,128)(2,1)S(1)}, bf16[2048,128]{1,0:T(8,128)(2,1)}, u32[]{:S(2)}) copy-start(bf16[2048,128]{1,0:T(8,128)(2,1)} %param.29) | copy-start | bytes 1572868
  26.2 29.6 %copy-start.9 = (bf16[128,2048]{1,0:T(8,128)(2,1)S(1)}, bf16[128,2048]{1,0:T(8,128)(2,1)}, u32[]{:S(2)}) copy-start(bf16[128,2048]{1,0:T(8,128)(2,1)} %param.30) | copy-start | bytes 1572868
  26.2 30.0 %copy-start.7 = (bf16[32,32,512]{2,1,0:T(8,128)(2,1)S(1)}, bf16[32,32,512]{2,1,0:T(8,128)(2,1)}, u32[]{:S(2)}) copy-start(bf16[32,32,512]{2,1,0:T(8,128)(2,1)} %param.24) | copy-start | bytes 3145732
  76.4 21.9 %all-to-all-start.2 = ((bf16[32,16,512]{2,1,0:T(8,128)(2,1)}), bf16[32,16,512]{2,1,0:T(8,128)(2,1)S(1)}, u32[]{:S(2)}, u32[]{:S(2)}) async-start(bf16[32,16,512]{2,1,0:T(8,128)(2,1)} %bitcast.35), calls=%async_computation.2 | async-start | bytes 1048576 | tf_op jit(solution)/shard_map/all_to_all | solution.py:443
  98.4 5.9 %copy-start.10 = (bf16[32,16,512]{2,1,0:T(8,128)(2,1)}, bf16[32,16,512]{2,1,0:T(8,128)(2,1)S(1)}, u32[]{:S(2)}) copy-start(bf16[32,16,512]{2,1,0:T(8,128)(2,1)S(1)} %all-to-all-done.2) | copy-start | bytes 1572868
  98.4 21.2 %all-to-all-start = ((bf16[32,16,512]{2,1,0:T(8,128)(2,1)}), bf16[32,16,512]{2,1,0:T(8,128)(2,1)S(1)}, u32[]{:S(2)}, u32[]{:S(2)}) async-start(bf16[32,16,512]{2,1,0:T(8,128)(2,1)} %bitcast.22), calls=%async_computation | async-start | bytes 1048576 | tf_op jit(solution)/shard_map/all_to_all | solution.py:443
  119.5 5.5 %copy-start.11 = (bf16[32,16,512]{2,1,0:T(8,128)(2,1)}, bf16[32,16,512]{2,1,0:T(8,128)(2,1)S(1)}, u32[]{:S(2)}) copy-start(bf16[32,16,512]{2,1,0:T(8,128)(2,1)S(1)} %all-to-all-done) | copy-start | bytes 1572868
  119.5 20.8 %all-to-all-start.3 = ((bf16[32,16,512]{2,1,0:T(8,128)(2,1)}), bf16[32,16,512]{2,1,0:T(8,128)(2,1)S(1)}, u32[]{:S(2)}, u32[]{:S(2)}) async-start(bf16[32,16,512]{2,1,0:T(8,128)(2,1)} %bitcast.85), calls=%async_computation.3 | async-start | bytes 1048576 | tf_op jit(solution)/shard_map/all_to_all | solution.py:445
  140.3 20.8 %all-to-all-start.1 = ((bf16[32,16,512]{2,1,0:T(8,128)(2,1)}), bf16[32,16,512]{2,1,0:T(8,128)(2,1)S(1)}, u32[]{:S(2)}, u32[]{:S(2)}) async-start(bf16[32,16,512]{2,1,0:T(8,128)(2,1)} %bitcast.86), calls=%async_computation.1 | async-start | bytes 1048576 | tf_op jit(solution)/shard_map/all_to_all | solution.py:445
where the time goes:
time: 166 us; the launch traced here: 163 us
  Pallas kernels  89 us (54%)
  starting transfers between devices  34.6 us (21%)
  waiting for transfers between devices  15.2 us (9%)
  local copies, waits for them, and re-layouts  12.1 us (7%)
  matrix products  7.82 us (5%)
  other arithmetic  4.28 us (3%)
    pallas_call x4, Pallas kernels, mixer(): pl.pallas_call(functools.partial(mixer_kernel, layout, feats // heads_cou...  59.7 us
    pallas_call x1, Pallas kernels, depthwise_stage(): pl.pallas_call(functools.partial(conv_kernel, row_count, col_count), out_...  18.9 us
    all_to_all x2, waiting for transfers between devices, split_sublayers(): lax.all_to_all(out.reshape(devices, -1, feats), ('row', 'col'), split_axi...  14.8 us
    all_to_all x2, starting transfers between devices, split_sublayers(): lax.all_to_all(out.reshape(devices, -1, feats), ('row', 'col'), split_axi...  11 us
    all_to_all x2, starting transfers between devices, split_sublayers(): lax.all_to_all(sent, ('row', 'col'), split_axis=0, concat_axis=0, tiled=T...  10.9 us
    pallas_call x2, Pallas kernels, axis_sum(): pl.pallas_call(functools.partial(axis_sum_kernel, axis, count), out_shape...  10.4 us
    dot_general x2, matrix products, key_major_bias(): spread = jnp.dot(table, chosen, precision=lax.Precision.HIGHEST)  4.84 us
    transpose x2, local copies, waits for them, and re-layouts, split_sublayers(): sent = section.reshape(row_fold, WIN, col_fold, pieces, count, feats).tra...  3.83 us
  transfers between devices with their start and end apart: 8, of which 3 were waited for; matrix products, arithmetic and copies ran while one was open for 7% of the time, Pallas kernels for 27%

commit v1 on v0

--- a/solution.py
+++ b/solution.py
@@ -451,6 +451,291 @@
             .reshape(row_fold, WIN, col_count, feats)
         )
     return jnp.stack(results, axis=1).reshape(row_count, col_count, feats)
+
+
+def device_of(flat, columns):
+    return {"row": lax.div(flat, columns), "col": lax.rem(flat, columns)}
+
+
+def exchange_kernel(
+    shape, head_size, x_ref, block_bias, grid_bias, gain_0, gain_1, gain_2, gain_3,
+    w0, w1, w2, w3, w4, w5, w6, w7, o_ref,
+    triple, heads, v0, v1, v2, v3, v4, v5, v6, v7,
+    section, got, output, back, weight_sem, send_sem, recv_sem,
+):
+    parts, pieces, columns, devices = shape
+    feats = x_ref.shape[1]
+    slabs = feats // LANES
+    per_slab = LANES // head_size
+    tokens = WIN * WIN
+    message = section.shape[1]
+    chunk = 256
+    batch = chunk // message
+    halves = devices // batch
+    part_rows = devices * message
+    me = lax.axis_index("row") * columns + lax.axis_index("col")
+    barrier = pltpu.get_barrier_semaphore()
+
+    def greet(step, carry):
+        pl.semaphore_signal(
+            barrier, inc=1, device_id=device_of(lax.rem(me + step, devices), columns),
+            device_id_type=pl.DeviceIdType.MESH,
+        )
+        return carry
+
+    lax.fori_loop(1, devices, greet, 0)
+    moves = [
+        pltpu.make_async_copy(src, dst, weight_sem.at[k])
+        for k, (src, dst) in enumerate(
+            zip((w0, w1, w2, w3, w4, w5, w6, w7), (v0, v1, v2, v3, v4, v5, v6, v7))
+        )
+    ]
+    for move in moves:
+        move.start()
+    for move in moves[:4]:
+        move.wait()
+
+    def project(values, rows, gain_ref, weight):
+        normed = normed_rows(values.astype(jnp.float32), gain_ref[...])
+        for part in range(3 * slabs // 2):
+            product = jnp.dot(
+                normed, weight[:, part * GROUP : (part + 1) * GROUP],
+                preferred_element_type=jnp.float32,
+            ).astype(jnp.bfloat16).astype(jnp.float32)
+            triple[2 * part, rows, :] = product[:, :LANES]
+            triple[2 * part + 1, rows, :] = product[:, LANES:]
+
+    lane = lax.broadcasted_iota(jnp.int32, (tokens, GROUP), 1)
+    head_of = (lane % LANES) // head_size
+    scale = head_size ** (-0.5)
+
+    def attend_window(spots, bias_ref):
+        def fetch(slab):
+            pieces = [triple[slab, spot, :] for spot in spots]
+            return pieces[0] if len(pieces) == 1 else jnp.concatenate(pieces, axis=0)
+
+        empty = jnp.zeros((tokens, LANES), jnp.bfloat16)
+        for group in range(slabs // 2):
+            first, second = 2 * group, 2 * group + 1
+            query_0 = fetch(first).astype(jnp.bfloat16)
+            query_1 = fetch(second).astype(jnp.bfloat16)
+            keys = jnp.concatenate([fetch(slabs + first), fetch(slabs + second)], axis=1)
+            vals = jnp.concatenate([fetch(2 * slabs + first), fetch(2 * slabs + second)], axis=1)
+            block_q = jnp.concatenate(
+                [
+                    jnp.concatenate([query_0, empty], axis=1),
+                    jnp.concatenate([empty, query_1], axis=1),
+                ],
+                axis=0,
+            )
+            block_k = jnp.concatenate(
+                [jnp.where(head_of == j, keys, 0.0).astype(jnp.bfloat16) for j in range(per_slab)],
+                axis=0,
+            )
+            block_v = jnp.concatenate(
+                [jnp.where(head_of == j, vals, 0.0).astype(jnp.bfloat16) for j in range(per_slab)],
+                axis=0,
+            )
+            scores = lax.dot_general(
+                block_k, block_q, (((1,), (1,)), ((), ())), preferred_element_type=jnp.float32
+            )
+            scores = (scores * scale + bias_ref[group]).reshape(per_slab, tokens, 2 * tokens)
+            weights = jnp.exp(scores - jnp.max(scores, axis=1, keepdims=True))
+            shares = weights * (1.0 / jnp.sum(weights, axis=1, keepdims=True))
+            shares = shares.reshape(per_slab * tokens, 2 * tokens).astype(jnp.bfloat16)
+            mixed = lax.dot_general(
+                shares, block_v, (((0,), (0,)), ((), ())), preferred_element_type=jnp.float32
+            )
+            for slab, part in (
+                (first, mixed[:tokens, :LANES]), (second, mixed[tokens:, LANES:])
+            ):
+                if len(spots) == 1:
+                    heads[slab, spots[0], :] = part
+                else:
+                    for r, spot in enumerate(spots):
+                        heads[slab, spot, :] = part[r * WIN : (r + 1) * WIN]
+
+    def feed(values, rows, gain_ref, out_w, up, down):
+        mixed = jnp.concatenate([heads[s, rows, :] for s in range(slabs)], axis=1).astype(jnp.bfloat16)
+        value = (
+            values.astype(jnp.float32)
+            + jnp.dot(mixed, out_w[...], preferred_element_type=jnp.float32)
+        ).astype(jnp.bfloat16).astype(jnp.float32)
+        normed = normed_rows(value, gain_ref[...])
+        tile = 512
+        for k in range(up.shape[1] // tile):
+            part = slice(k * tile, (k + 1) * tile)
+            hidden = jax.nn.gelu(
+                jnp.dot(normed, up[:, part], preferred_element_type=jnp.float32),
+                approximate=True,
+            ).astype(jnp.bfloat16)
+            value = value + jnp.dot(hidden, down[part, :], preferred_element_type=jnp.float32)
+        return value.astype(jnp.bfloat16)
+
+    def block_step(step, carry):
+        base = pl.multiple_of(step * chunk, chunk)
+        whole = pl.ds(0, chunk)
+        project(x_ref[pl.ds(base, chunk), :], whole, gain_0, v0)
+
+        def attend_pair(piece, inner):
+            for fold in range(message // WIN):
+                start = piece * (WIN * message) + fold * WIN
+                attend_window(
+                    [pl.ds(pl.multiple_of(start + r * message, WIN), WIN) for r in range(WIN)],
+                    block_bias,
+                )
+            return inner
+
+        lax.fori_loop(0, batch // WIN, attend_pair, 0)
+        done = feed(x_ref[pl.ds(base, chunk), :], whole, gain_1, v1, v2, v3)
+        section[pl.ds(step * batch, batch)] = done.reshape(batch, message, feats)
+
+        @pl.when(step == 0)
+        def _():
+            pl.semaphore_wait(barrier, devices - 1)
+
+        part, half = lax.div(step, halves), lax.rem(step, halves)
+
+        def send(i, inner):
+            at = lax.rem(i + me, batch)
+            target = lax.rem(at, WIN) * pieces + half * (batch // WIN) + lax.div(at, WIN)
+            src, dst = section.at[step * batch + at], got.at[part * devices + me]
+
+            @pl.when(target != me)
+            def _():
+                pltpu.make_async_remote_copy(
+                    src_ref=src, dst_ref=dst, send_sem=send_sem.at[0, part],
+                    recv_sem=recv_sem.at[0, part], device_id=device_of(target, columns),
+                    device_id_type=pl.DeviceIdType.MESH,
+                ).start()
+
+            @pl.when(target == me)
+            def _():
+                pltpu.make_async_copy(src, dst, recv_sem.at[0, part]).start()
+
+            return inner
+
+        lax.fori_loop(0, batch, send, 0)
+        return carry
+
+    lax.fori_loop(0, parts * halves, block_step, 0)
+    for move in moves[4:]:
+        move.wait()
+    slot = lax.rem(me, pieces) * WIN + lax.div(me, pieces)
+
+    def arrived(buffer, kind, part):
+        block = buffer.at[pl.ds(part * devices, devices)]
+        pltpu.make_async_copy(block, block, recv_sem.at[kind, part]).wait()
+
+    def grid_step(part, carry):
+        arrived(got, 0, part)
+
+        def rows_of(half):
+            return got[pl.ds(part * devices + half * batch, batch)].reshape(chunk, feats)
+
+        for half in range(halves):
+            project(rows_of(half), pl.ds(half * chunk, chunk), gain_2, v4)
+
+        def attend_pair(pair, inner):
+            for k in range(2):
+                attend_window([pl.ds(2 * pair + k, tokens, stride=WIN)], grid_bias)
+            return inner
+
+        lax.fori_loop(0, part_rows // tokens // 2, attend_pair, 0)
+
+        def feed_half(half, inner):
+            rows = pl.ds(pl.multiple_of(half * chunk, chunk), chunk)
+            done = feed(rows_of(half), rows, gain_3, v5, v6, v7)
+            output[pl.ds(part * devices + half * batch, batch)] = done.reshape(batch, message, feats)
+
+            def send(i, inner_2):
+                target = half * batch + lax.rem(i + me, batch)
+                src, dst = output.at[part * devices + target], back.at[part * devices + slot]
+
+                @pl.when(target != me)
+                def _():
+                    pltpu.make_async_remote_copy(
+                        src_ref=src, dst_ref=dst, send_sem=send_sem.at[1, part],
+                        recv_sem=recv_sem.at[1, part], device_id=device_of(target, columns),
+                        device_id_type=pl.DeviceIdType.MESH,
+                    ).start()
+
+                @pl.when(target == me)
+                def _():
+                    pltpu.make_async_copy(src, dst, recv_sem.at[1, part]).start()
+
+                return inner_2
+
+            lax.fori_loop(0, batch, send, 0)
+            return inner
+
+        lax.fori_loop(0, halves, feed_half, 0)
+        return carry
+
+    lax.fori_loop(0, parts, grid_step, 0)
+    fold_rows = parts * WIN
+    width = pieces * WIN
+
+    def finish(part, carry):
+        arrived(back, 1, part)
+
+        def place(down, inner):
+            tiles = [
+                back[part * devices + piece * WIN + down].astype(jnp.float32)
+                for piece in range(pieces)
+            ]
+            for fold in range(message // WIN):
+                line = jnp.concatenate([t[fold * WIN : (fold + 1) * WIN] for t in tiles], axis=0)
+                start = (fold * fold_rows + part * WIN + down) * width
+                o_ref[pl.ds(pl.multiple_of(start, width), width), :] = line.astype(jnp.bfloat16)
+            return inner
+
+        return lax.fori_loop(0, WIN, place, carry)
+
+    lax.fori_loop(0, parts, finish, 0)
+    for kind, buffer in ((0, section), (1, output)):
+        for part in range(parts):
+            sent = buffer.at[pl.ds(part * devices, devices - 1)]
+            pltpu.make_async_copy(sent, sent, send_sem.at[kind, part]).wait()
+
+
+def exchange(x, shape, head_size, block_bias, grid_bias, gains, weights):
+    parts, pieces, columns, devices = shape
+    rows, feats = x.shape
+    message = rows // (parts * devices)
+    part_rows = rows // parts
+    vmem = pl.BlockSpec(memory_space=pltpu.VMEM)
+    hbm = pl.BlockSpec(memory_space=pltpu.HBM)
+    mail = pltpu.VMEM((parts * devices, message, feats), jnp.bfloat16)
+    return pl.pallas_call(
+        functools.partial(exchange_kernel, shape, head_size),
+        out_shape=jax.ShapeDtypeStruct((rows, feats), jnp.bfloat16),
+        in_specs=[vmem] * 7 + [hbm] * 8,
+        out_specs=vmem,
+        scratch_shapes=[
+            pltpu.VMEM((3 * feats // LANES, part_rows, LANES), jnp.float32),
+            pltpu.VMEM((feats // LANES, part_rows, LANES), jnp.float32),
+        ]
+        + [pltpu.VMEM(w.shape, jnp.bfloat16) for w in weights]
+        + [
+            mail, mail, mail, mail,
+            pltpu.SemaphoreType.DMA((8,)),
+            pltpu.SemaphoreType.DMA((2, parts)),
+            pltpu.SemaphoreType.DMA((2, parts)),
+        ],
+        compiler_params=pltpu.CompilerParams(
+            collective_id=3, has_side_effects=True, vmem_limit_bytes=48 * 1024 * 1024
+        ),
+        name="exchange",
+    )(x, block_bias, grid_bias, *[g[None] for g in gains], *weights)
+
+
+def compact(row_count, col_count):
+    row_devices, col_devices = lax.axis_size("row"), lax.axis_size("col")
+    return (
+        2 * row_devices == WIN and col_devices == WIN
+        and row_count % (2 * WIN) == 0 and col_count == WIN * row_devices
+    )
 
 
 PAD = 8
@@ -601,6 +886,25 @@
             second_expand, second_reduce, grid_table.shape[0],
         )
 
+    if compact(row_count, col_count):
+        parts, pieces = row_count // (2 * WIN), col_count // WIN
+        plain = np.arange(WIN * WIN)
+        block_bias = key_major_bias(block_table, plain // WIN, plain % WIN)
+        grid_bias = key_major_bias(
+            grid_table, 2 * (plain // (2 * col_devices)) + plain % 2, plain // 2 % col_devices
+        )
+        ordered = (
+            conv_out.reshape(2, parts, WIN, pieces, WIN, channels)
+            .transpose(1, 3, 2, 0, 4, 5)
+            .reshape(-1, channels)
+        )
+        return exchange(
+            ordered, (parts, pieces, col_devices, row_devices * col_devices),
+            channels // block_table.shape[0], block_bias, grid_bias,
+            (block_gain, first_gain, grid_gain, second_gain),
+            (block_projection, block_output, first_expand, first_reduce,
+             grid_projection, grid_output, second_expand, second_reduce),
+        ).reshape(row_count, col_count, channels)
     return split_sublayers(conv_out, run_block, run_grid, block_table, grid_table)
 
 

time: 166 us -> 125 us (0.75); the launches traced: 163 us -> 124 us
  starting transfers between devices: 34.6 us -> 12.5 us
  waiting for transfers between devices: 15.2 us -> 0.01 us
  Pallas kernels: 89 us -> 92 us
  local copies, waits for them, and re-layouts: 12.1 us -> 9.12 us
  other arithmetic: 4.28 us -> 2.17 us
    all_to_all x4 -> x0, starting transfers between devices: 21.9 us -> none  [the longest x2 11 us: split_sublayers(): lax.all_to_all(out.reshape(devices, -1, feats), ('row', 'col'), split_axi...]
    all_to_all x4 -> x0, waiting for transfers between devices: 15.1 us -> none  [the longest x2 14.8 us: split_sublayers(): lax.all_to_all(out.reshape(devices, -1, feats), ('row', 'col'), split_axi...]
    transpose x4 -> x0, local copies, waits for them, and re-layouts: 4.75 us -> none  [the longest x2 3.83 us: split_sublayers(): sent = section.reshape(row_fold, WIN, col_fold, pieces, count, feats).tra...]
    pallas_call x4 -> x1, Pallas kernels: 59.7 us -> 62.6 us  [exchange(): pl.pallas_call(functools.partial(exchange_kernel, shape, head_size), out_...]
    unnamed x26 -> x37, local copies, waits for them, and re-layouts: 0.16 us -> 2.46 us
    another operation x1 -> x0, other arithmetic: 2.11 us -> none  [split_sublayers(): return jnp.stack(results, axis=1).reshape(row_count, col_count, feats)]
  transfers between devices with their start and end apart: 8 -> 4, of which waited for: 3 -> 0; matrix products, arithmetic and copies ran while one was open for 7% -> 8% of each run, Pallas kernels for 27% -> 0%
where the time goes in v1:
time: 125 us; the launch traced here: 124 us
  Pallas kernels  92 us (74%)
  starting transfers between devices  12.5 us (10%)
  local copies, waits for them, and re-layouts  9.12 us (7%)
  matrix products  7.82 us (6%)
  other arithmetic  2.17 us (2%)
    pallas_call x1, Pallas kernels, exchange(): pl.pallas_call(functools.partial(exchange_kernel, shape, head_size), out_...  62.6 us
    pallas_call x1, Pallas kernels, depthwise_stage(): pl.pallas_call(functools.partial(conv_kernel, row_count, col_count), out_...  19 us
    pallas_call x2, Pallas kernels, axis_sum(): pl.pallas_call(functools.partial(axis_sum_kernel, axis, count), out_shape...  10.4 us
    dot_general x2, matrix products, key_major_bias(): spread = jnp.dot(table, chosen, precision=lax.Precision.HIGHEST)  4.84 us
    ppermute x1, starting transfers between devices, extended(): lax.ppermute(tail, axis, [(i, (i + 1) % count) for i in range(ends)])  3.24 us
    ppermute x1, starting transfers between devices, depthwise_stage(): right = lax.ppermute(tall[:, :1], 'col', [(b, a) for a, b in ahead])  3.13 us
    ppermute x1, starting transfers between devices, depthwise_stage(): left = lax.ppermute(tall[:, col_count - 1:], 'col', ahead)  3.1 us
    ppermute x1, starting transfers between devices, extended(): lax.ppermute(head, axis, [((i + 1) % count, i) for i in range(ends)])  3.06 us
  transfers between devices with their start and end apart: 4, of which 0 were waited for; matrix products, arithmetic and copies ran while one was open for 8% of the time, Pallas kernels for 0%

profile of v1, /device:TPU:5, one launch (start us, length us, event | category | flops | bytes accessed | tf_op | source)
XLA Modules:
  0.0 124.1 jit_solution(17907186613744520019)
XLA Ops:
  0.0 0.9 fusion.12
  0.9 3.2 %collective-permute-start = (bf16[1,32,512]{2,1,0:T(8,128)(2,1)S(1)}, bf16[1,32,512]{2,1,0:T(8,128)(2,1)S(1)}, u32[]{:S(2)}, u32[]{:S(2)}) collective-permute-start(bf16[1,32,512]{2,1,0:T(8,128)(2,1)S(1)} %get-tuple-element.12), channel_id=1, source_target_pairs={{0,8},{8,16},{16,24},{1,9},{9,17},{17,25},{2,10},{10,18},{18,26},{... | collective-permute-start | bytes 98312 | tf_op jit(solution)/shard_map/ppermute | solution.py:22
  4.2 3.1 %collective-permute-start.1 = (bf16[1,32,512]{2,1,0:T(8,128)(2,1)S(1)}, bf16[1,32,512]{2,1,0:T(8,128)(2,1)S(1)}, u32[]{:S(2)}, u32[]{:S(2)}) collective-permute-start(bf16[1,32,512]{2,1,0:T(8,128)(2,1)S(1)} %get-tuple-element.11), channel_id=1, source_target_pairs={{8,0},{16,8},{24,16},{9,1},{17,9},{25,17},{10,2},{18,10},{26,18},{... | collective-permute-start | bytes 98312 | tf_op jit(solution)/shard_map/ppermute | solution.py:24
  7.3 2.8 %convolution_bitcast_fusion.1 = f32[16,4096]{1,0:T(8,128)} fusion(f32[16,225]{1,0:T(8,128)} %param.35, s32[4096]{0:T(1024)} %constant.27.clone), kind=kOutput, calls=%fused_computation.2 | convolution fusion | flops 177868800 | bytes 292928 | tf_op jit(solution)/shard_map/dot_general | solution.py:401
  10.0 2.1 %convolution_bitcast_fusion = f32[16,4096]{1,0:T(8,128)S(1)} fusion(f32[16,225]{1,0:T(8,128)} %param.42, s32[4096]{0:T(1024)} %constant.28.clone), kind=kOutput, calls=%fused_computation.1 | convolution fusion | flops 177868800 | bytes 292928 | tf_op jit(solution)/shard_map/dot_general | solution.py:401
  12.1 0.1 constant_dynamic-update-slice_fusion.1
  12.3 0.9 fusion.11
  13.2 3.1 %collective-permute-start.2 = (bf16[34,1,512]{2,1,0:T(2,128)(2,1)}, bf16[34,1,512]{2,1,0:T(2,128)(2,1)}, u32[]{:S(2)}, u32[]{:S(2)}) collective-permute-start(bf16[34,1,512]{2,1,0:T(2,128)(2,1)} %get-tuple-element.9), channel_id=1, source_target_pairs={{1,0},{2,1},{3,2},{4,3},{5,4},{6,5},{7,6},{9,8},{10,9},{11,10},{12... | collective-permute-start | bytes 104456 | tf_op jit(solution)/shard_map/ppermute | solution.py:815
  16.3 3.1 %collective-permute-start.3 = (bf16[34,1,512]{2,1,0:T(2,128)(2,1)}, bf16[34,1,512]{2,1,0:T(2,128)(2,1)}, u32[]{:S(2)}, u32[]{:S(2)}) collective-permute-start(bf16[34,1,512]{2,1,0:T(2,128)(2,1)} %get-tuple-element.10), channel_id=1, source_target_pairs={{0,1},{1,2},{2,3},{3,4},{4,5},{5,6},{6,7},{8,9},{9,10},{10,11},{11... | collective-permute-start | bytes 104456 | tf_op jit(solution)/shard_map/ppermute | solution.py:814
  19.4 0.1 add_convert_fusion.flags
  19.5 1.1 reshape.52
  20.7 0.4 copy.31
  21.1 0.3 reshape.53.block_bias
  21.4 0.2 reshape.54
  21.6 0.0 copy-start.5
  21.6 1.2 copy.30
  22.8 1.3 %reshape.55.grid_bias = f32[2,256,128]{2,1,0:T(8,128)S(1)} reshape(f32[2,4,64,2,64]{4,3,2,1,0:T(2,128)} %bitcast.55) | data formatting | bytes 524288 | tf_op jit(solution)/shard_map/reshape | solution.py:405
  24.2 0.1 pad.2.clone
  24.3 2.1 %pad_maximum_fusion = bf16[34,40,512]{2,1,0:T(8,128)(2,1)S(1)} fusion(bf16[34,1,512]{2,1,0:T(2,128)(2,1)} %collective-permute-done.3, bf16[34,1,512]{2,1,0:T(2,128)(2,1)} %collective-permute-done.2, bf16[34,32,512]{2,1,0:T(8,128)(2,1)} %copy-done.12, bf16[40]{0:T(256)(128)(2,1)S(1)} %pad.2.clone), kind=kLoop, calls=%fused_computation.11 | loop fusion | flops 5570560 | bytes 2576464 | tf_op jit(solution)/shard_map/concatenate | solution.py:817
  26.4 0.0 copy-start.14
  26.4 19.0 %conv_stage.1 = (bf16[1024,2048]{1,0:T(8,128)(2,1)S(1)}, f32[1,2048]{1,0:T(1,128)S(1)}) custom-call(f32[4]{0:T(128)S(1)} %add_convert_fusion.flags, bf16[1360,512]{1,0:T(8,128)(2,1)S(1)} %bitcast.44, f32[1,512]{1,0:T(1,128)S(1)} %bitcast.48, f32[1,512]{1,0:T(1,128)S(1)} %bitcast.49, bf16[512,2048]{1,0:T(8,128)(2,1)S(1)} %copy-done.1, f32[9,2048]{1,0:T(8,128)S(1)} %copy-done.5), custom_call_target="tpu_custom_call" | custom-call | tf_op jit(solution)/shard_map/conv_stage/pallas_call | solution.py:820
  45.5 3.5 %axis_sum_row.1.x_ref = f32[16,128]{1,0:T(8,128)S(1)} custom-call(f32[16,128]{1,0:T(8,128)S(1)} %bitcast.47), custom_call_target="tpu_custom_call" | custom-call | tf_op jit(solution)/shard_map/axis_sum_row/pallas_call | solution.py:210
  49.0 6.9 %axis_sum_col.1 = f32[16,128]{1,0:T(8,128)S(1)} custom-call(f32[16,128]{1,0:T(8,128)S(1)} %axis_sum_row.1.x_ref), custom_call_target="tpu_custom_call" | custom-call | tf_op jit(solution)/shard_map/axis_sum_col/pallas_call | solution.py:210
  55.9 0.3 convolution_bitcast_fusion.2
  56.2 0.3 fusion.5
  56.6 2.3 %fusion.2 = bf16[1024,512]{1,0:T(8,128)(2,1)S(1)} fusion(bf16[1024,512]{1,0:T(8,128)(2,1)S(1)} %bitcast.56, bf16[2048,512]{1,0:T(8,128)(2,1)S(1)} %copy-done, bf16[1024,2048]{1,0:T(8,128)(2,1)S(1)} %get-tuple-element.7, f32[2048]{0:T(1024)S(1)} %add_divide_fusion), kind=kOutput, calls=%fused_computation.8 | convolution fusion | flops 2155347968 | bytes 8396800 | tf_op jit(solution)/shard_map/dot_general | solution.py:874
  58.9 0.0 copy-start.2
  59.0 0.1 copy.25
  59.2 1.2 copy-done.2
  60.4 0.1 copy-done.3
  60.5 62.6 %exchange.1 = bf16[1024,512]{1,0:T(8,128)(2,1)S(1)} custom-call(bf16[1024,512]{1,0:T(8,128)(2,1)S(1)} %bitcast.45, f32[2,256,128]{2,1,0:T(8,128)S(1)} %reshape.53.block_bias, f32[2,256,128]{2,1,0:T(8,128)S(1)} %reshape.55.grid_bias, f32[1,512]{1,0:T(1,128)S(1)} %bitcast.50, f32[1,512]{1,0:T(1,128)S(1)} %bitcast.51, f32[1,512]{1,0:T(1,128)S(1)} %bitcast.52, ...), custom_call_target="tpu_custom_call" | custom-call | tf_op jit(solution)/shard_map/exchange/pallas_call | solution.py:710
  123.1 1.0 copy.35
  (38 shorter events, 0.1 us)
Async XLA Ops:
  0.0 56.6 %copy-start = (bf16[2048,512]{1,0:T(8,128)(2,1)S(1)}, bf16[2048,512]{1,0:T(8,128)(2,1)}, u32[]{:S(2)}) copy-start(bf16[2048,512]{1,0:T(8,128)(2,1)} %param.31) | copy-start | bytes 6291460
  0.0 12.1 %copy-start.13 = (bf16[32,32,512]{2,1,0:T(8,128)(2,1)S(1)}, bf16[32,32,512]{2,1,0:T(8,128)(2,1)}, u32[]{:S(2)}) copy-start(bf16[32,32,512]{2,1,0:T(8,128)(2,1)} %param.24) | copy-start | bytes 3145732
  0.9 11.2 %collective-permute-start = (bf16[1,32,512]{2,1,0:T(8,128)(2,1)S(1)}, bf16[1,32,512]{2,1,0:T(8,128)(2,1)S(1)}, u32[]{:S(2)}, u32[]{:S(2)}) collective-permute-start(bf16[1,32,512]{2,1,0:T(8,128)(2,1)S(1)} %get-tuple-element.12), channel_id=1, source_target_pairs={{0,8},{8,16},{16,24},{1,9},{9,17},{17,25},{2,10},{10,18},{18,26},{... | collective-permute-start | bytes 98312 | tf_op jit(solution)/shard_map/ppermute | solution.py:22
  4.2 8.0 %collective-permute-start.1 = (bf16[1,32,512]{2,1,0:T(8,128)(2,1)S(1)}, bf16[1,32,512]{2,1,0:T(8,128)(2,1)S(1)}, u32[]{:S(2)}, u32[]{:S(2)}) collective-permute-start(bf16[1,32,512]{2,1,0:T(8,128)(2,1)S(1)} %get-tuple-element.11), channel_id=1, source_target_pairs={{8,0},{16,8},{24,16},{9,1},{17,9},{25,17},{10,2},{18,10},{26,18},{... | collective-permute-start | bytes 98312 | tf_op jit(solution)/shard_map/ppermute | solution.py:24
  12.2 7.2 %copy-start.12 = (bf16[34,32,512]{2,1,0:T(8,128)(2,1)}, bf16[34,32,512]{2,1,0:T(8,128)(2,1)S(1)}, u32[]{:S(2)}) copy-start(bf16[34,32,512]{2,1,0:T(8,128)(2,1)S(1)} %constant_dynamic-update-slice_fusion) | copy-start | bytes 3342340
  13.2 11.1 %collective-permute-start.2 = (bf16[34,1,512]{2,1,0:T(2,128)(2,1)}, bf16[34,1,512]{2,1,0:T(2,128)(2,1)}, u32[]{:S(2)}, u32[]{:S(2)}) collective-permute-start(bf16[34,1,512]{2,1,0:T(2,128)(2,1)} %get-tuple-element.9), channel_id=1, source_target_pairs={{1,0},{2,1},{3,2},{4,3},{5,4},{6,5},{7,6},{9,8},{10,9},{11,10},{12... | collective-permute-start | bytes 104456 | tf_op jit(solution)/shard_map/ppermute | solution.py:815
  16.3 8.0 %collective-permute-start.3 = (bf16[34,1,512]{2,1,0:T(2,128)(2,1)}, bf16[34,1,512]{2,1,0:T(2,128)(2,1)}, u32[]{:S(2)}, u32[]{:S(2)}) collective-permute-start(bf16[34,1,512]{2,1,0:T(2,128)(2,1)} %get-tuple-element.10), channel_id=1, source_target_pairs={{0,1},{1,2},{2,3},{3,4},{4,5},{5,6},{6,7},{8,9},{9,10},{10,11},{11... | collective-permute-start | bytes 104456 | tf_op jit(solution)/shard_map/ppermute | solution.py:814
  21.6 4.8 %copy-start.5 = (f32[9,2048]{1,0:T(8,128)S(1)}, f32[9,2048]{1,0:T(8,128)}, u32[]{:S(2)}) copy-start(f32[9,2048]{1,0:T(8,128)} %taps_ref.1) | copy-start | bytes 221188
  21.6 4.8 %copy-start.6 = (f32[512]{0:T(512)S(1)}, f32[512]{0:T(512)}, u32[]{:S(2)}) copy-start(f32[512]{0:T(512)} %param.25) | copy-start | bytes 6148
  21.6 4.8 %copy-start.7 = (f32[512]{0:T(512)S(1)}, f32[512]{0:T(512)}, u32[]{:S(2)}) copy-start(f32[512]{0:T(512)} %param.26) | copy-start | bytes 6148
  24.2 2.2 %copy-start.1 = (bf16[512,2048]{1,0:T(8,128)(2,1)S(1)}, bf16[512,2048]{1,0:T(8,128)(2,1)}, u32[]{:S(2)}) copy-start(bf16[512,2048]{1,0:T(8,128)(2,1)} %expand_ref.1) | copy-start | bytes 6291460
  26.4 29.5 %copy-start.15 = (bf16[2048,128]{1,0:T(8,128)(2,1)S(1)}, bf16[2048,128]{1,0:T(8,128)(2,1)}, u32[]{:S(2)}) copy-start(bf16[2048,128]{1,0:T(8,128)(2,1)} %param.29) | copy-start | bytes 1572868
  26.4 29.8 %copy-start.16 = (bf16[128,2048]{1,0:T(8,128)(2,1)S(1)}, bf16[128,2048]{1,0:T(8,128)(2,1)}, u32[]{:S(2)}) copy-start(bf16[128,2048]{1,0:T(8,128)(2,1)} %param.30) | copy-start | bytes 1572868
  26.4 30.2 %copy-start.14 = (bf16[32,32,512]{2,1,0:T(8,128)(2,1)S(1)}, bf16[32,32,512]{2,1,0:T(8,128)(2,1)}, u32[]{:S(2)}) copy-start(bf16[32,32,512]{2,1,0:T(8,128)(2,1)} %param.24) | copy-start | bytes 3145732
  56.6 2.6 %copy-start.4 = (bf16[512,512]{1,0:T(8,128)(2,1)S(1)}, bf16[512,512]{1,0:T(8,128)(2,1)}, u32[]{:S(2)}) copy-start(bf16[512,512]{1,0:T(8,128)(2,1)} %w5.1) | copy-start | bytes 1572868
  58.9 1.4 %copy-start.2 = (bf16[512,1536]{1,0:T(8,128)(2,1)S(1)}, bf16[512,1536]{1,0:T(8,128)(2,1)}, u32[]{:S(2)}) copy-start(bf16[512,1536]{1,0:T(8,128)(2,1)} %w0.1) | copy-start | bytes 4718596
  59.0 1.5 %copy-start.3 = (bf16[512,512]{1,0:T(8,128)(2,1)S(1)}, bf16[512,512]{1,0:T(8,128)(2,1)}, u32[]{:S(2)}) copy-start(bf16[512,512]{1,0:T(8,128)(2,1)} %w1.1) | copy-start | bytes 1572868
  59.0 1.5 %copy-start.8 = (f32[512]{0:T(512)S(1)}, f32[512]{0:T(512)}, u32[]{:S(2)}) copy-start(f32[512]{0:T(512)} %param.32) | copy-start | bytes 6148
  59.0 1.5 %copy-start.9 = (f32[512]{0:T(512)S(1)}, f32[512]{0:T(512)}, u32[]{:S(2)}) copy-start(f32[512]{0:T(512)} %param.36) | copy-start | bytes 6148
  59.0 1.5 %copy-start.10 = (f32[512]{0:T(512)S(1)}, f32[512]{0:T(512)}, u32[]{:S(2)}) copy-start(f32[512]{0:T(512)} %param.39) | copy-start | bytes 6148
  59.0 1.5 %copy-start.11 = (f32[512]{0:T(512)S(1)}, f32[512]{0:T(512)}, u32[]{:S(2)}) copy-start(f32[512]{0:T(512)} %param.43) | copy-start | bytes 6148

commit v2 on v1

--- a/solution.py
+++ b/solution.py
@@ -9,6 +9,7 @@
 from jax.sharding import PartitionSpec as P
 
 WIN = 8
+PAD = 8
 
 
 def extended(cells, sides, width):
@@ -457,29 +458,58 @@
     return {"row": lax.div(flat, columns), "col": lax.rem(flat, columns)}
 
 
-def exchange_kernel(
-    shape, head_size, x_ref, block_bias, grid_bias, gain_0, gain_1, gain_2, gain_3,
-    w0, w1, w2, w3, w4, w5, w6, w7, o_ref,
-    triple, heads, v0, v1, v2, v3, v4, v5, v6, v7,
-    section, got, output, back, weight_sem, send_sem, recv_sem,
+CORNERS = ((-1, -1), (-1, 1), (1, -1), (1, 1))
+
+
+def split_parts(values):
+    high = values.astype(jnp.bfloat16)
+    rest = values - high.astype(jnp.float32)
+    middle = rest.astype(jnp.bfloat16)
+    low = (rest - middle.astype(jnp.float32)).astype(jnp.bfloat16)
+    return high, middle, low
+
+
+def exact_rows(values, weight):
+    stacked = jnp.concatenate([p.astype(jnp.float32) for p in split_parts(values)], axis=0)
+    product = jnp.dot(
+        stacked.astype(jnp.bfloat16), weight[...], preferred_element_type=jnp.float32
+    )
+    return jnp.sum(product, axis=0, keepdims=True)
+
+
+def block_kernel(
+    shape, head_size, latent, scale_in, shift_in, taps_in, block_table, grid_table,
+    gain_0, gain_1, gain_2, gain_3,
+    h0, h1, h2, h3, w0, w1, w2, w3, w4, w5, w6, w7, o_ref,
+    u0, u1, u2, u3, triple, heads, v0, v1, v2, v3, v4, v5, v6, v7,
+    section, got, output, back, edges, halo, corner, conv_in, halo_in, expanded, deep_ref,
+    sums, slots, excite_ref, padded, block_bias, grid_bias,
+    weight_sem, send_sem, recv_sem, halo_send, halo_recv, sum_send, sum_recv,
 ):
-    parts, pieces, columns, devices = shape
-    feats = x_ref.shape[1]
+    parts, pieces, rows_n, columns = shape
+    devices = rows_n * columns
+    row_count, col_count, feats = latent.shape
+    width = u0.shape[1]
     slabs = feats // LANES
     per_slab = LANES // head_size
     tokens = WIN * WIN
     message = section.shape[1]
+    folds = message // WIN
     chunk = 256
     batch = chunk // message
     halves = devices // batch
     part_rows = devices * message
-    me = lax.axis_index("row") * columns + lax.axis_index("col")
+    wide = col_count + PAD
+    fold_rows = row_count // folds
+    row_at, col_at = lax.axis_index("row"), lax.axis_index("col")
+    me = row_at * columns + col_at
+    mesh_ids = pl.DeviceIdType.MESH
     barrier = pltpu.get_barrier_semaphore()
 
     def greet(step, carry):
         pl.semaphore_signal(
             barrier, inc=1, device_id=device_of(lax.rem(me + step, devices), columns),
-            device_id_type=pl.DeviceIdType.MESH,
+            device_id_type=mesh_ids,
         )
         return carry
 
@@ -487,12 +517,236 @@
     moves = [
         pltpu.make_async_copy(src, dst, weight_sem.at[k])
         for k, (src, dst) in enumerate(
-            zip((w0, w1, w2, w3, w4, w5, w6, w7), (v0, v1, v2, v3, v4, v5, v6, v7))
+            zip(
+                (h0, h1, h2, h3, w0, w1, w2, w3, w4, w5, w6, w7),
+                (u0, u1, u2, u3, v0, v1, v2, v3, v4, v5, v6, v7),
+            )
         )
     ]
     for move in moves:
         move.start()
-    for move in moves[:4]:
+
+    near = {
+        (down, side): jnp.logical_and(
+            jnp.logical_and(row_at + down >= 0, row_at + down < rows_n),
+            jnp.logical_and(col_at + side >= 0, col_at + side < columns),
+        )
+        for down in (-1, 0, 1)
+        for side in (-1, 0, 1)
+    }
+    for side, block, inner in ((0, 0, 0), (1, col_count - message, message - 1)):
+        for group in range(row_count // 8):
+            cells = latent[8 * group : 8 * group + 8, block : block + message, :]
+            edges[side, 8 * group : 8 * group + 8, :] = (
+                cells.astype(jnp.float32)[:, inner, :].astype(jnp.bfloat16)
+            )
+    sides = ((-1, 0), (1, 0), (0, -1), (0, 1))
+    for k, way in enumerate(sides):
+
+        @pl.when(jnp.logical_not(near[way]))
+        def _(k=k):
+            halo[k] = jnp.zeros(halo.shape[1:], halo.dtype)
+
+    for k, way in enumerate(CORNERS):
+
+        @pl.when(jnp.logical_not(near[way]))
+        def _(k=k):
+            corner[k] = jnp.zeros(corner.shape[1:], corner.dtype)
+
+    for group in range(row_count // 8):
+        cells = latent[8 * group : 8 * group + 8].reshape(8 * col_count, feats)
+        conv_in[8 * group * col_count : 8 * (group + 1) * col_count, :] = (
+            cells.astype(jnp.float32) * scale_in[...] + shift_in[...]
+        ).astype(jnp.bfloat16)
+    pl.semaphore_wait(barrier, devices - 1)
+
+    def outgoing(k):
+        if k < 4:
+            down, side = sides[k]
+            src = (
+                latent.at[0], latent.at[row_count - 1], edges.at[0], edges.at[1]
+            )[k]
+            dst = halo.at[k ^ 1]
+        else:
+            down, side = CORNERS[k - 4]
+            line = 0 if down < 0 else row_count - 1
+            start = 0 if side < 0 else col_count - message
+            src = latent.at[line, pl.ds(start, message)]
+            dst = corner.at[7 - k]
+        return pltpu.make_async_remote_copy(
+            src_ref=src, dst_ref=dst, send_sem=halo_send.at[k], recv_sem=halo_recv.at[k],
+            device_id={"row": row_at + down, "col": col_at + side}, device_id_type=mesh_ids,
+        )
+
+    ways = sides + CORNERS
+    for k, way in enumerate(ways):
+
+        @pl.when(near[way])
+        def _(k=k):
+            outgoing(k).start()
+
+    moves[0].wait()
+    block = 256
+
+    def expand(step, carry):
+        lanes = pl.ds(pl.multiple_of(step * block, block), block)
+        for group in range(row_count // 8):
+            product = jnp.dot(
+                conv_in[8 * group * col_count : 8 * (group + 1) * col_count, :], u0[:, lanes],
+                preferred_element_type=jnp.float32,
+            )
+            value = jax.nn.gelu(product, approximate=True).astype(jnp.bfloat16).astype(jnp.float32)
+            for r in range(8):
+                start = (1 + 8 * group + r) * wide
+                for half in range(block // LANES):
+                    expanded[step * (block // LANES) + half, start : start + col_count, :] = value[
+                        r * col_count : (r + 1) * col_count, half * LANES : (half + 1) * LANES
+                    ]
+        return carry
+
+    lax.fori_loop(0, width // block, expand, 0)
+    for k, way in enumerate(ways):
+        opposite = (-way[0], -way[1])
+        src_k = ways.index(opposite)
+
+        @pl.when(near[way])
+        def _(k=k, src_k=src_k):
+            target = halo.at[k] if k < 4 else corner.at[k - 4]
+            pltpu.make_async_copy(target, target, halo_recv.at[src_k]).wait()
+
+    picked = [
+        corner[k].astype(jnp.float32)[(message - 1 if side < 0 else 0) :][:1]
+        for k, (_, side) in enumerate(CORNERS)
+    ]
+    picked = jnp.concatenate(picked + [jnp.zeros((message - 4, feats), jnp.float32)], axis=0)
+    around = 2 * (row_count + col_count)
+    for k, (start, size) in enumerate(
+        (
+            (0, col_count), (col_count, col_count), (2 * col_count, row_count),
+            (2 * col_count + row_count, row_count),
+        )
+    ):
+        halo_in[start : start + size, :] = (
+            halo[k].astype(jnp.float32) * scale_in[...] + shift_in[...]
+        ).astype(jnp.bfloat16)
+    halo_in[around:, :] = (picked * scale_in[...] + shift_in[...]).astype(jnp.bfloat16)
+    tall = row_count + 2
+
+    def expand_halo(step, carry):
+        lanes = pl.ds(pl.multiple_of(step * block, block), block)
+        product = jnp.dot(halo_in[...], u0[:, lanes], preferred_element_type=jnp.float32)
+        value = jax.nn.gelu(product, approximate=True).astype(jnp.bfloat16).astype(jnp.float32)
+        up = jnp.where(near[(-1, 0)], value[:col_count], 0.0)
+        low = jnp.where(near[(1, 0)], value[col_count : 2 * col_count], 0.0)
+        left = jnp.where(near[(0, -1)], value[2 * col_count : 2 * col_count + row_count], 0.0)
+        right = jnp.where(near[(0, 1)], value[2 * col_count + row_count : around], 0.0)
+        for half in range(block // LANES):
+            inner = slice(half * LANES, (half + 1) * LANES)
+            outer = step * (block // LANES) + half
+            last = (tall - 1) * wide
+            expanded[outer, 0:col_count, :] = up[:, inner]
+            expanded[outer, last : last + col_count, :] = low[:, inner]
+            expanded[outer, pl.ds(wide + col_count, row_count, stride=wide), :] = right[:, inner]
+            expanded[outer, pl.ds(2 * wide - 1, row_count, stride=wide), :] = left[:, inner]
+            for k, way in enumerate(CORNERS):
+                row = (0 if way[0] < 0 else last) + (wide - 1 if way[1] < 0 else col_count)
+                expanded[outer, row : row + 1, :] = jnp.where(
+                    near[way], value[around + k : around + k + 1, inner], 0.0
+                )
+        return carry
+
+    lax.fori_loop(0, width // block, expand_halo, 0)
+
+    def depth(step, carry):
+        lanes = pl.ds(pl.multiple_of(step * LANES, LANES), LANES)
+        taps = [taps_in[k : k + 1, lanes] for k in range(9)]
+
+        def pair_of_rows(group, total):
+            results = []
+            for fold in range(folds):
+                first = fold * fold_rows + 2 * group
+                held = [
+                    expanded[step, pl.ds(pl.multiple_of((first + k) * wide, 8), wide), :]
+                    for k in range(4)
+                ]
+                for k in range(2):
+                    sums_of = [
+                        held[k] * taps[side]
+                        + held[k + 1] * taps[3 + side]
+                        + held[k + 2] * taps[6 + side]
+                        for side in range(3)
+                    ]
+                    summed = (
+                        pltpu.roll(sums_of[0], 1, 0) + sums_of[1] + pltpu.roll(sums_of[2], wide - 1, 0)
+                    )[:col_count]
+                    value = jax.nn.gelu(summed, approximate=True)
+                    total = total + jnp.sum(value.reshape(col_count // 8, 8, LANES), axis=0)
+                    results.append(value)
+            part, down = lax.div(2 * group, WIN), lax.rem(2 * group, WIN)
+            for k in range(2):
+                for piece in range(pieces):
+                    rows = slice(piece * WIN, (piece + 1) * WIN)
+                    tile = jnp.concatenate(
+                        [results[2 * fold + k][rows] for fold in range(folds)], axis=0
+                    )
+                    at = part * devices + piece * WIN + down + k
+                    deep_ref[at, :, lanes] = tile.astype(jnp.bfloat16)
+            return total
+
+        sums[:, lanes] = lax.fori_loop(
+            0, fold_rows // 2, pair_of_rows, jnp.zeros((8, LANES), jnp.float32)
+        )
+        return carry
+
+    lax.fori_loop(0, width // LANES, depth, 0)
+    for move in moves[1:4]:
+        move.wait()
+    slots[me] = exact_rows(sums[...], u1)
+
+    def share(step, carry):
+        pltpu.make_async_remote_copy(
+            src_ref=slots.at[me], dst_ref=slots.at[me], send_sem=sum_send, recv_sem=sum_recv,
+            device_id=device_of(lax.rem(me + step, devices), columns), device_id_type=mesh_ids,
+        ).start()
+        return carry
+
+    lax.fori_loop(1, devices, share, 0)
+    span = 2 * WIN
+    spot = lax.broadcasted_iota(jnp.int32, (slabs * per_slab, span * span), 1)
+    place = lax.broadcasted_iota(jnp.int32, (WIN, LANES), 1)
+    for table, bias in ((block_table, block_bias), (grid_table, grid_bias)):
+        padded[...] = jnp.zeros(padded.shape, jnp.float32)
+        padded[:, : table.shape[1]] = table[...]
+        flat = padded[...]
+        spread = jnp.zeros(flat.shape, jnp.float32)
+        for down in range(2 * WIN - 1):
+            moved = flat if down == 0 else pltpu.roll(flat, down, 1)
+            spread = jnp.where(spot // span == down, moved, spread)
+        for head in range(slabs * per_slab // 2):
+            group, j = head // per_slab, head % per_slab
+            pair = [
+                jnp.broadcast_to(spread[h : h + 1], (WIN, span * span))
+                for h in (group * 2 * per_slab + j, group * 2 * per_slab + per_slab + j)
+            ]
+            for kr in range(WIN):
+                shift = span * kr - (span * (WIN - 1) + WIN - 1)
+                first, second = [
+                    pltpu.roll(
+                        pair[s], (shift + WIN * s) % (span * span), 1, stride=1, stride_axis=0
+                    )[:, :LANES]
+                    for s in range(2)
+                ]
+                start = j * tokens + kr * WIN
+                bias[group, start : start + WIN, :] = jnp.where(place % span < WIN, first, second)
+    arrivals = slots.at[pl.ds(0, devices - 1)]
+    pltpu.make_async_copy(arrivals, arrivals, sum_recv).wait()
+    pooled = jnp.sum(slots[...].reshape(devices, LANES), axis=0, keepdims=True) / (
+        row_count * rows_n * col_count * columns
+    )
+    reduced = jax.nn.silu(pooled)
+    spare = jnp.zeros((7, LANES), jnp.float32)
+    excite_ref[...] = jax.nn.sigmoid(exact_rows(jnp.concatenate([reduced, spare], axis=0), u2))
+    for move in moves[4:8]:
         move.wait()
 
     def project(values, rows, gain_ref, weight):
@@ -511,23 +765,23 @@
 
     def attend_window(spots, bias_ref):
         def fetch(slab):
-            pieces = [triple[slab, spot, :] for spot in spots]
-            return pieces[0] if len(pieces) == 1 else jnp.concatenate(pieces, axis=0)
-
-        empty = jnp.zeros((tokens, LANES), jnp.bfloat16)
+            return [triple[slab, spot, :] for spot in spots]
+
+        def whole(slab):
+            return jnp.concatenate(fetch(slab), axis=0)
+
+        empty = jnp.zeros((WIN, LANES), jnp.float32)
         for group in range(slabs // 2):
             first, second = 2 * group, 2 * group + 1
-            query_0 = fetch(first).astype(jnp.bfloat16)
-            query_1 = fetch(second).astype(jnp.bfloat16)
-            keys = jnp.concatenate([fetch(slabs + first), fetch(slabs + second)], axis=1)
-            vals = jnp.concatenate([fetch(2 * slabs + first), fetch(2 * slabs + second)], axis=1)
             block_q = jnp.concatenate(
                 [
-                    jnp.concatenate([query_0, empty], axis=1),
-                    jnp.concatenate([empty, query_1], axis=1),
+                    jnp.concatenate([p for q in fetch(first) for p in (q, empty)], axis=0),
+                    jnp.concatenate([p for q in fetch(second) for p in (empty, q)], axis=0),
                 ],
-                axis=0,
-            )
+                axis=1,
+            ).astype(jnp.bfloat16)
+            keys = jnp.concatenate([whole(slabs + first), whole(slabs + second)], axis=1)
+            vals = jnp.concatenate([whole(2 * slabs + first), whole(2 * slabs + second)], axis=1)
             block_k = jnp.concatenate(
                 [jnp.where(head_of == j, keys, 0.0).astype(jnp.bfloat16) for j in range(per_slab)],
                 axis=0,
@@ -546,14 +800,10 @@
             mixed = lax.dot_general(
                 shares, block_v, (((0,), (0,)), ((), ())), preferred_element_type=jnp.float32
             )
-            for slab, part in (
-                (first, mixed[:tokens, :LANES]), (second, mixed[tokens:, LANES:])
-            ):
-                if len(spots) == 1:
-                    heads[slab, spots[0], :] = part
-                else:
-                    for r, spot in enumerate(spots):
-                        heads[slab, spot, :] = part[r * WIN : (r + 1) * WIN]
+            for r, spot in enumerate(spots):
+                start = 2 * r * WIN
+                heads[first, spot, :] = mixed[start : start + WIN, :LANES]
+                heads[second, spot, :] = mixed[start + WIN : start + 2 * WIN, LANES:]
 
     def feed(values, rows, gain_ref, out_w, up, down):
         mixed = jnp.concatenate([heads[s, rows, :] for s in range(slabs)], axis=1).astype(jnp.bfloat16)
@@ -573,12 +823,32 @@
         return value.astype(jnp.bfloat16)
 
     def block_step(step, carry):
-        base = pl.multiple_of(step * chunk, chunk)
+        part, half = lax.div(step, halves), lax.rem(step, halves)
         whole = pl.ds(0, chunk)
-        project(x_ref[pl.ds(base, chunk), :], whole, gain_0, v0)
+        across = batch // WIN
+        own = {}
+        for down in range(WIN):
+            for fold in range(folds):
+                line = latent[
+                    fold * fold_rows + part * WIN + down,
+                    pl.ds(pl.multiple_of(half * (across * WIN), across * WIN), across * WIN), :,
+                ].astype(jnp.float32)
+                for piece in range(across):
+                    own[piece, down, fold] = line[piece * WIN : (piece + 1) * WIN]
+        own = jnp.concatenate([own[key] for key in sorted(own)], axis=0)
+        for k in range(width // block):
+            lanes = slice(k * block, (k + 1) * block)
+            gated = (
+                deep_ref[pl.ds(step * batch, batch), :, lanes].reshape(chunk, block).astype(jnp.float32)
+                * excite_ref[:, lanes]
+            ).astype(jnp.bfloat16)
+            own = own + jnp.dot(gated, u3[lanes, :], preferred_element_type=jnp.float32)
+        value = own.astype(jnp.bfloat16)
+        conv_in[0:chunk, :] = value
+        project(value, whole, gain_0, v0)
 
         def attend_pair(piece, inner):
-            for fold in range(message // WIN):
+            for fold in range(folds):
                 start = piece * (WIN * message) + fold * WIN
                 attend_window(
                     [pl.ds(pl.multiple_of(start + r * message, WIN), WIN) for r in range(WIN)],
@@ -586,19 +856,13 @@
                 )
             return inner
 
-        lax.fori_loop(0, batch // WIN, attend_pair, 0)
-        done = feed(x_ref[pl.ds(base, chunk), :], whole, gain_1, v1, v2, v3)
+        lax.fori_loop(0, across, attend_pair, 0)
+        done = feed(conv_in[0:chunk, :], whole, gain_1, v1, v2, v3)
         section[pl.ds(step * batch, batch)] = done.reshape(batch, message, feats)
-
-        @pl.when(step == 0)
-        def _():
-            pl.semaphore_wait(barrier, devices - 1)
-
-        part, half = lax.div(step, halves), lax.rem(step, halves)
 
         def send(i, inner):
             at = lax.rem(i + me, batch)
-            target = lax.rem(at, WIN) * pieces + half * (batch // WIN) + lax.div(at, WIN)
+            target = lax.rem(at, WIN) * pieces + half * across + lax.div(at, WIN)
             src, dst = section.at[step * batch + at], got.at[part * devices + me]
 
             @pl.when(target != me)
@@ -606,7 +870,7 @@
                 pltpu.make_async_remote_copy(
                     src_ref=src, dst_ref=dst, send_sem=send_sem.at[0, part],
                     recv_sem=recv_sem.at[0, part], device_id=device_of(target, columns),
-                    device_id_type=pl.DeviceIdType.MESH,
+                    device_id_type=mesh_ids,
                 ).start()
 
             @pl.when(target == me)
@@ -619,13 +883,13 @@
         return carry
 
     lax.fori_loop(0, parts * halves, block_step, 0)
-    for move in moves[4:]:
+    for move in moves[8:]:
         move.wait()
     slot = lax.rem(me, pieces) * WIN + lax.div(me, pieces)
 
     def arrived(buffer, kind, part):
-        block = buffer.at[pl.ds(part * devices, devices)]
-        pltpu.make_async_copy(block, block, recv_sem.at[kind, part]).wait()
+        mail = buffer.at[pl.ds(part * devices, devices)]
+        pltpu.make_async_copy(mail, mail, recv_sem.at[kind, part]).wait()
 
     def grid_step(part, carry):
         arrived(got, 0, part)
@@ -638,7 +902,14 @@
 
         def attend_pair(pair, inner):
             for k in range(2):
-                attend_window([pl.ds(2 * pair + k, tokens, stride=WIN)], grid_bias)
+                attend_window(
+                    [
+                        pl.ds(r * columns * message + fold * WIN + 2 * pair + k, columns, stride=message)
+                        for r in range(rows_n)
+                        for fold in range(folds)
+                    ],
+                    grid_bias,
+                )
             return inner
 
         lax.fori_loop(0, part_rows // tokens // 2, attend_pair, 0)
@@ -657,7 +928,7 @@
                     pltpu.make_async_remote_copy(
                         src_ref=src, dst_ref=dst, send_sem=send_sem.at[1, part],
                         recv_sem=recv_sem.at[1, part], device_id=device_of(target, columns),
-                        device_id_type=pl.DeviceIdType.MESH,
+                        device_id_type=mesh_ids,
                     ).start()
 
                 @pl.when(target == me)
@@ -673,61 +944,88 @@
         return carry
 
     lax.fori_loop(0, parts, grid_step, 0)
-    fold_rows = parts * WIN
-    width = pieces * WIN
 
     def finish(part, carry):
         arrived(back, 1, part)
 
-        def place(down, inner):
+        def put(down, inner):
             tiles = [
                 back[part * devices + piece * WIN + down].astype(jnp.float32)
                 for piece in range(pieces)
             ]
-            for fold in range(message // WIN):
+            for fold in range(folds):
                 line = jnp.concatenate([t[fold * WIN : (fold + 1) * WIN] for t in tiles], axis=0)
-                start = (fold * fold_rows + part * WIN + down) * width
-                o_ref[pl.ds(pl.multiple_of(start, width), width), :] = line.astype(jnp.bfloat16)
+                o_ref[fold * fold_rows + part * WIN + down] = line.astype(jnp.bfloat16)
             return inner
 
-        return lax.fori_loop(0, WIN, place, carry)
+        return lax.fori_loop(0, WIN, put, carry)
 
     lax.fori_loop(0, parts, finish, 0)
     for kind, buffer in ((0, section), (1, output)):
         for part in range(parts):
             sent = buffer.at[pl.ds(part * devices, devices - 1)]
             pltpu.make_async_copy(sent, sent, send_sem.at[kind, part]).wait()
-
-
-def exchange(x, shape, head_size, block_bias, grid_bias, gains, weights):
-    parts, pieces, columns, devices = shape
-    rows, feats = x.shape
+    pltpu.make_async_copy(arrivals, arrivals, sum_send).wait()
+    for k, way in enumerate(ways):
+
+        @pl.when(near[way])
+        def _(k=k):
+            target = halo.at[k] if k < 4 else corner.at[k - 4]
+            pltpu.make_async_copy(target, target, halo_send.at[k]).wait()
+
+
+def whole_block(latent, scale, shift, taps, tables, gains, front, weights):
+    row_count, col_count, feats = latent.shape
+    rows_n, columns = lax.axis_size("row"), lax.axis_size("col")
+    devices = rows_n * columns
+    parts, pieces = row_count // (2 * WIN), col_count // WIN
+    heads_n = tables[0].shape[0]
+    rows = row_count * col_count
+    width = front[0].shape[1]
     message = rows // (parts * devices)
-    part_rows = rows // parts
+    around = 2 * (row_count + col_count) + message
     vmem = pl.BlockSpec(memory_space=pltpu.VMEM)
     hbm = pl.BlockSpec(memory_space=pltpu.HBM)
-    mail = pltpu.VMEM((parts * devices, message, feats), jnp.bfloat16)
+    half_type = jnp.bfloat16
+    mail = pltpu.VMEM((parts * devices, message, feats), half_type)
+    bias = pltpu.VMEM((heads_n // 8, 4 * WIN * WIN, 2 * WIN * WIN), jnp.float32)
+    dma = pltpu.SemaphoreType.DMA
     return pl.pallas_call(
-        functools.partial(exchange_kernel, shape, head_size),
-        out_shape=jax.ShapeDtypeStruct((rows, feats), jnp.bfloat16),
-        in_specs=[vmem] * 7 + [hbm] * 8,
+        functools.partial(block_kernel, (parts, pieces, rows_n, columns), feats // heads_n),
+        out_shape=jax.ShapeDtypeStruct(latent.shape, half_type),
+        in_specs=[vmem] * 10 + [hbm] * 12,
         out_specs=vmem,
-        scratch_shapes=[
-            pltpu.VMEM((3 * feats // LANES, part_rows, LANES), jnp.float32),
-            pltpu.VMEM((feats // LANES, part_rows, LANES), jnp.float32),
+        scratch_shapes=[pltpu.VMEM(w.shape, half_type) for w in front]
+        + [
+            pltpu.VMEM((3 * feats // LANES, rows // parts, LANES), jnp.float32),
+            pltpu.VMEM((feats // LANES, rows // parts, LANES), jnp.float32),
         ]
-        + [pltpu.VMEM(w.shape, jnp.bfloat16) for w in weights]
+        + [pltpu.VMEM(w.shape, half_type) for w in weights]
         + [
             mail, mail, mail, mail,
-            pltpu.SemaphoreType.DMA((8,)),
-            pltpu.SemaphoreType.DMA((2, parts)),
-            pltpu.SemaphoreType.DMA((2, parts)),
+            pltpu.VMEM((2, row_count, feats), half_type),
+            pltpu.VMEM((4, row_count, feats), half_type),
+            pltpu.VMEM((4, message, feats), half_type),
+            pltpu.VMEM((rows, feats), half_type),
+            pltpu.VMEM((around, feats), half_type),
+            pltpu.VMEM(
+                (width // LANES, (row_count + 2) * (col_count + PAD), LANES), jnp.float32
+            ),
+            pltpu.VMEM((parts * devices, message, width), half_type),
+            pltpu.VMEM((8, width), jnp.float32),
+            pltpu.VMEM((devices, 1, LANES), jnp.float32),
+            pltpu.VMEM((1, width), jnp.float32),
+            pltpu.VMEM((heads_n, 4 * WIN * WIN), jnp.float32),
+            bias, bias,
+            dma((12,)), dma((2, parts)), dma((2, parts)), dma((8,)), dma((8,)), dma, dma,
         ],
         compiler_params=pltpu.CompilerParams(
-            collective_id=3, has_side_effects=True, vmem_limit_bytes=48 * 1024 * 1024
+            collective_id=3, has_side_effects=True, vmem_limit_bytes=60 * 1024 * 1024
         ),
-        name="exchange",
-    )(x, block_bias, grid_bias, *[g[None] for g in gains], *weights)
+        name="whole_block",
+    )(
+        latent, scale[None], shift[None], taps, *tables, *[g[None] for g in gains], *front, *weights
+    )
 
 
 def compact(row_count, col_count):
@@ -735,10 +1033,8 @@
     return (
         2 * row_devices == WIN and col_devices == WIN
         and row_count % (2 * WIN) == 0 and col_count == WIN * row_devices
-    )
-
-
-PAD = 8
+        and row_count == col_count
+    )
 
 
 def conv_kernel(
@@ -861,6 +1157,14 @@
     row_devices = lax.axis_size("row")
     col_devices = lax.axis_size("col")
     row_count, col_count, channels = latent.shape
+    if compact(row_count, col_count) and squeeze_up.shape[0] == LANES:
+        return whole_block(
+            latent, conv_scale, conv_shift, depth_kernel, (block_table, grid_table),
+            (block_gain, first_gain, grid_gain, second_gain),
+            (expand_weight, squeeze_down, squeeze_up, project_weight),
+            (block_projection, block_output, first_expand, first_reduce,
+             grid_projection, grid_output, second_expand, second_reduce),
+        )
     depthwise, local_sums = depthwise_stage(
         latent, conv_scale, conv_shift, expand_weight, depth_kernel
     )
@@ -886,25 +1190,6 @@
             second_expand, second_reduce, grid_table.shape[0],
         )
 
-    if compact(row_count, col_count):
-        parts, pieces = row_count // (2 * WIN), col_count // WIN
-        plain = np.arange(WIN * WIN)
-        block_bias = key_major_bias(block_table, plain // WIN, plain % WIN)
-        grid_bias = key_major_bias(
-            grid_table, 2 * (plain // (2 * col_devices)) + plain % 2, plain // 2 % col_devices
-        )
-        ordered = (
-            conv_out.reshape(2, parts, WIN, pieces, WIN, channels)
-            .transpose(1, 3, 2, 0, 4, 5)
-            .reshape(-1, channels)
-        )
-        return exchange(
-            ordered, (parts, pieces, col_devices, row_devices * col_devices),
-            channels // block_table.shape[0], block_bias, grid_bias,
-            (block_gain, first_gain, grid_gain, second_gain),
-            (block_projection, block_output, first_expand, first_reduce,
-             grid_projection, grid_output, second_expand, second_reduce),
-        ).reshape(row_count, col_count, channels)
     return split_sublayers(conv_out, run_block, run_grid, block_table, grid_table)
 
 

time: 125 us -> 94.9 us (0.76)
  starting transfers between devices: 12.5 us -> 0 us
  matrix products: 7.82 us -> 0 us
  local copies, waits for them, and re-layouts: 9.12 us -> 2.3 us
  other arithmetic: 2.17 us -> 0 us
    ppermute x4 -> x0, starting transfers between devices: 12.5 us -> none  [the longest x1 3.24 us: extended(): lax.ppermute(tail, axis, [(i, (i + 1) % count) for i in range(ends)])]
    dot_general x5 -> x0, matrix products: 7.82 us -> none  [the longest x2 4.84 us: key_major_bias(): spread = jnp.dot(table, chosen, precision=lax.Precision.HIGHEST)]
    reshape x6 -> x0, local copies, waits for them, and re-layouts: 4.6 us -> none  [the longest x4 2.96 us: key_major_bias(): spread.reshape(head_count // 8, 2, 4, tokens, tokens)]
    concatenate x1 -> x0, other arithmetic: 2.07 us -> none  [depthwise_stage(): ext = jnp.concatenate([tall, right, blank, left], axis=1).reshape(-1, feats)]
    slice x2 -> x0, local copies, waits for them, and re-layouts: 1.84 us -> none  [the longest x1 0.94 us: extended(): head = lax.slice_in_dim(cells, 0, width, axis=dim)]
    pallas_call x4 -> x1, Pallas kernels: 92 us -> 92.5 us  [whole_block(): pl.pallas_call(functools.partial(block_kernel, (parts, pieces, rows_n, co...]
  transfers between devices with their start and end apart: 4 -> 0, of which waited for: 0 -> 0; matrix products, arithmetic and copies ran while one was open for 8% -> 0% of each run, Pallas kernels for 0% -> 0%
where the time goes in v2:
time: 94.9 us; the launch traced here: 94.8 us
  Pallas kernels  92.5 us (97%)
  local copies, waits for them, and re-layouts  2.3 us (2%)
    pallas_call x1, Pallas kernels, whole_block(): pl.pallas_call(functools.partial(block_kernel, (parts, pieces, rows_n, co...  92.5 us
    unnamed x1, local copies, waits for them, and re-layouts  2.3 us

profile of v2, /device:TPU:5, one launch (start us, length us, event | category | flops | bytes accessed | tf_op | source)
XLA Modules:
  0.0 94.8 jit_solution(1693661594659757346)
XLA Ops:
  0.0 92.5 %whole_block.1 = bf16[32,32,512]{2,1,0:T(8,128)(2,1)} custom-call(bf16[32,32,512]{2,1,0:T(8,128)(2,1)} %latent.1, f32[1,512]{1,0:T(1,128)} %bitcast.6, f32[1,512]{1,0:T(1,128)} %bitcast.7, f32[9,2048]{1,0:T(8,128)} %taps_in.1, f32[16,225]{1,0:T(8,128)} %block_table.1, f32[16,225]{1,0:T(8,128)} %grid_table.1, f32[1,512]{1,0:T(1,128)} %bitcast.8, ...), custom_call_target="tpu_custom_call" | custom-call | tf_op jit(solution)/shard_map/whole_block/pallas_call | solution.py:993
  92.5 2.3 %copy.24 = bf16[32,32,512]{2,1,0:T(8,128)(2,1)} copy(bf16[32,32,512]{2,1,0:T(8,128)(2,1)} %whole_block.1) | data formatting | bytes 2097152

commit v3 on v2

--- a/solution.py
+++ b/solution.py
@@ -10,6 +10,8 @@
 
 WIN = 8
 PAD = 8
+QUAD = 4
+LOG2E = 1.4426950408889634
 
 
 def extended(cells, sides, width):
@@ -477,13 +479,18 @@
     return jnp.sum(product, axis=0, keepdims=True)
 
 
+def twice_gelu(x):
+    inner = x * (0.7978845608028654 + (0.7978845608028654 * 0.044715) * (x * x))
+    return x + x * jnp.tanh(inner)
+
+
 def block_kernel(
     shape, head_size, latent, scale_in, shift_in, taps_in, block_table, grid_table,
     gain_0, gain_1, gain_2, gain_3,
     h0, h1, h2, h3, w0, w1, w2, w3, w4, w5, w6, w7, o_ref,
     u0, u1, u2, u3, triple, heads, v0, v1, v2, v3, v4, v5, v6, v7,
     section, got, output, back, edges, halo, corner, conv_in, halo_in, expanded, deep_ref,
-    sums, slots, excite_ref, padded, block_bias, grid_bias,
+    sums, slots, excite_ref, padded, block_bias, grid_bias, score_ref, share_ref,
     weight_sem, send_sem, recv_sem, halo_send, halo_recv, sum_send, sum_recv,
 ):
     parts, pieces, rows_n, columns = shape
@@ -595,9 +602,9 @@
                 conv_in[8 * group * col_count : 8 * (group + 1) * col_count, :], u0[:, lanes],
                 preferred_element_type=jnp.float32,
             )
-            value = jax.nn.gelu(product, approximate=True).astype(jnp.bfloat16).astype(jnp.float32)
+            value = twice_gelu(product).astype(jnp.bfloat16).astype(jnp.float32)
             for r in range(8):
-                start = (1 + 8 * group + r) * wide
+                start = PAD + (1 + 8 * group + r) * wide
                 for half in range(block // LANES):
                     expanded[step * (block // LANES) + half, start : start + col_count, :] = value[
                         r * col_count : (r + 1) * col_count, half * LANES : (half + 1) * LANES
@@ -635,7 +642,7 @@
     def expand_halo(step, carry):
         lanes = pl.ds(pl.multiple_of(step * block, block), block)
         product = jnp.dot(halo_in[...], u0[:, lanes], preferred_element_type=jnp.float32)
-        value = jax.nn.gelu(product, approximate=True).astype(jnp.bfloat16).astype(jnp.float32)
+        value = twice_gelu(product).astype(jnp.bfloat16).astype(jnp.float32)
         up = jnp.where(near[(-1, 0)], value[:col_count], 0.0)
         low = jnp.where(near[(1, 0)], value[col_count : 2 * col_count], 0.0)
         left = jnp.where(near[(0, -1)], value[2 * col_count : 2 * col_count + row_count], 0.0)
@@ -643,13 +650,13 @@
         for half in range(block // LANES):
             inner = slice(half * LANES, (half + 1) * LANES)
             outer = step * (block // LANES) + half
-            last = (tall - 1) * wide
-            expanded[outer, 0:col_count, :] = up[:, inner]
+            last = PAD + (tall - 1) * wide
+            expanded[outer, PAD : PAD + col_count, :] = up[:, inner]
             expanded[outer, last : last + col_count, :] = low[:, inner]
-            expanded[outer, pl.ds(wide + col_count, row_count, stride=wide), :] = right[:, inner]
-            expanded[outer, pl.ds(2 * wide - 1, row_count, stride=wide), :] = left[:, inner]
+            expanded[outer, pl.ds(PAD + wide + col_count, row_count, stride=wide), :] = right[:, inner]
+            expanded[outer, pl.ds(PAD + wide - 1, row_count, stride=wide), :] = left[:, inner]
             for k, way in enumerate(CORNERS):
-                row = (0 if way[0] < 0 else last) + (wide - 1 if way[1] < 0 else col_count)
+                row = (PAD if way[0] < 0 else last) + (-1 if way[1] < 0 else col_count)
                 expanded[outer, row : row + 1, :] = jnp.where(
                     near[way], value[around + k : around + k + 1, inner], 0.0
                 )
@@ -659,27 +666,27 @@
 
     def depth(step, carry):
         lanes = pl.ds(pl.multiple_of(step * LANES, LANES), LANES)
-        taps = [taps_in[k : k + 1, lanes] for k in range(9)]
+        taps = [0.5 * taps_in[k : k + 1, lanes] for k in range(9)]
 
         def pair_of_rows(group, total):
             results = []
             for fold in range(folds):
                 first = fold * fold_rows + 2 * group
+                base = pl.multiple_of(first * wide, 8)
                 held = [
-                    expanded[step, pl.ds(pl.multiple_of((first + k) * wide, 8), wide), :]
+                    [
+                        expanded[step, pl.ds(base + (PAD + k * wide + side), col_count), :]
+                        for side in (-1, 0, 1)
+                    ]
                     for k in range(4)
                 ]
                 for k in range(2):
-                    sums_of = [
-                        held[k] * taps[side]
-                        + held[k + 1] * taps[3 + side]
-                        + held[k + 2] * taps[6 + side]
+                    summed = sum(
+                        held[k + down][side] * taps[3 * down + side]
+                        for down in range(3)
                         for side in range(3)
-                    ]
-                    summed = (
-                        pltpu.roll(sums_of[0], 1, 0) + sums_of[1] + pltpu.roll(sums_of[2], wide - 1, 0)
-                    )[:col_count]
-                    value = jax.nn.gelu(summed, approximate=True)
+                    )
+                    value = twice_gelu(summed)
                     total = total + jnp.sum(value.reshape(col_count // 8, 8, LANES), axis=0)
                     results.append(value)
             part, down = lax.div(2 * group, WIN), lax.rem(2 * group, WIN)
@@ -701,7 +708,7 @@
     lax.fori_loop(0, width // LANES, depth, 0)
     for move in moves[1:4]:
         move.wait()
-    slots[me] = exact_rows(sums[...], u1)
+    slots[me] = exact_rows(0.5 * sums[...], u1)
 
     def share(step, carry):
         pltpu.make_async_remote_copy(
@@ -716,7 +723,7 @@
     place = lax.broadcasted_iota(jnp.int32, (WIN, LANES), 1)
     for table, bias in ((block_table, block_bias), (grid_table, grid_bias)):
         padded[...] = jnp.zeros(padded.shape, jnp.float32)
-        padded[:, : table.shape[1]] = table[...]
+        padded[:, : table.shape[1]] = table[...] * LOG2E
         flat = padded[...]
         spread = jnp.zeros(flat.shape, jnp.float32)
         for down in range(2 * WIN - 1):
@@ -745,7 +752,7 @@
     )
     reduced = jax.nn.silu(pooled)
     spare = jnp.zeros((7, LANES), jnp.float32)
-    excite_ref[...] = jax.nn.sigmoid(exact_rows(jnp.concatenate([reduced, spare], axis=0), u2))
+    excite_ref[...] = 0.5 * jax.nn.sigmoid(exact_rows(jnp.concatenate([reduced, spare], axis=0), u2))
     for move in moves[4:8]:
         move.wait()
 
@@ -760,50 +767,57 @@
             triple[2 * part + 1, rows, :] = product[:, LANES:]
 
     lane = lax.broadcasted_iota(jnp.int32, (tokens, GROUP), 1)
-    head_of = (lane % LANES) // head_size
-    scale = head_size ** (-0.5)
-
-    def attend_window(spots, bias_ref):
-        def fetch(slab):
-            return [triple[slab, spot, :] for spot in spots]
-
-        def whole(slab):
-            return jnp.concatenate(fetch(slab), axis=0)
-
-        empty = jnp.zeros((WIN, LANES), jnp.float32)
-        for group in range(slabs // 2):
-            first, second = 2 * group, 2 * group + 1
-            block_q = jnp.concatenate(
+    masks = [
+        jnp.where((lane % LANES) // head_size == j, 1.0, 0.0).astype(jnp.bfloat16)
+        for j in range(per_slab)
+    ]
+    scale = head_size ** (-0.5) * LOG2E
+
+    def attend_windows(windows, bias_ref):
+        def spread(spots, slab, group):
+            joined = jnp.concatenate(
                 [
-                    jnp.concatenate([p for q in fetch(first) for p in (q, empty)], axis=0),
-                    jnp.concatenate([p for q in fetch(second) for p in (empty, q)], axis=0),
+                    jnp.concatenate([triple[slab + 2 * group + k, spot, :] for spot in spots], axis=0)
+                    for k in range(2)
                 ],
                 axis=1,
             ).astype(jnp.bfloat16)
-            keys = jnp.concatenate([whole(slabs + first), whole(slabs + second)], axis=1)
-            vals = jnp.concatenate([whole(2 * slabs + first), whole(2 * slabs + second)], axis=1)
-            block_k = jnp.concatenate(
-                [jnp.where(head_of == j, keys, 0.0).astype(jnp.bfloat16) for j in range(per_slab)],
-                axis=0,
+            return jnp.concatenate([joined * mask for mask in masks], axis=0)
+
+        empty = jnp.zeros((WIN, LANES), jnp.float32)
+        chains = [(n, g) for n in range(len(windows)) for g in range(slabs // 2)]
+        for at, (n, group) in enumerate(chains):
+            spots = windows[n]
+            left, right = [
+                [triple[2 * group + k, spot, :] for spot in spots] for k in range(2)
+            ]
+            block_q = jnp.concatenate(
+                [
+                    jnp.concatenate([p for q in left for p in (q, empty)], axis=0),
+                    jnp.concatenate([p for q in right for p in (empty, q)], axis=0),
+                ],
+                axis=1,
+            ).astype(jnp.bfloat16)
+            score_ref[at] = lax.dot_general(
+                spread(spots, slabs, group), block_q, (((1,), (1,)), ((), ())),
+                preferred_element_type=jnp.float32,
             )
-            block_v = jnp.concatenate(
-                [jnp.where(head_of == j, vals, 0.0).astype(jnp.bfloat16) for j in range(per_slab)],
-                axis=0,
+        for at, (n, group) in enumerate(chains):
+            scores = (score_ref[at] * scale + bias_ref[group]).reshape(
+                per_slab, tokens, 2 * tokens
             )
-            scores = lax.dot_general(
-                block_k, block_q, (((1,), (1,)), ((), ())), preferred_element_type=jnp.float32
+            weights = jnp.exp2(scores - jnp.max(scores, axis=1, keepdims=True))
+            shares = weights * (1.0 / jnp.sum(weights, axis=1, keepdims=True))
+            share_ref[at] = shares.reshape(per_slab * tokens, 2 * tokens).astype(jnp.bfloat16)
+        for at, (n, group) in enumerate(chains):
+            mixed = lax.dot_general(
+                share_ref[at], spread(windows[n], 2 * slabs, group), (((0,), (0,)), ((), ())),
+                preferred_element_type=jnp.float32,
             )
-            scores = (scores * scale + bias_ref[group]).reshape(per_slab, tokens, 2 * tokens)
-            weights = jnp.exp(scores - jnp.max(scores, axis=1, keepdims=True))
-            shares = weights * (1.0 / jnp.sum(weights, axis=1, keepdims=True))
-            shares = shares.reshape(per_slab * tokens, 2 * tokens).astype(jnp.bfloat16)
-            mixed = lax.dot_general(
-                shares, block_v, (((0,), (0,)), ((), ())), preferred_element_type=jnp.float32
-            )
-            for r, spot in enumerate(spots):
+            for r, spot in enumerate(windows[n]):
                 start = 2 * r * WIN
-                heads[first, spot, :] = mixed[start : start + WIN, :LANES]
-                heads[second, spot, :] = mixed[start + WIN : start + 2 * WIN, LANES:]
+                heads[2 * group, spot, :] = mixed[start : start + WIN, :LANES]
+                heads[2 * group + 1, spot, :] = mixed[start + WIN : start + 2 * WIN, LANES:]
 
     def feed(values, rows, gain_ref, out_w, up, down):
         mixed = jnp.concatenate([heads[s, rows, :] for s in range(slabs)], axis=1).astype(jnp.bfloat16)
@@ -813,13 +827,15 @@
         ).astype(jnp.bfloat16).astype(jnp.float32)
         normed = normed_rows(value, gain_ref[...])
         tile = 512
+        total = None
         for k in range(up.shape[1] // tile):
             part = slice(k * tile, (k + 1) * tile)
-            hidden = jax.nn.gelu(
-                jnp.dot(normed, up[:, part], preferred_element_type=jnp.float32),
-                approximate=True,
+            hidden = twice_gelu(
+                jnp.dot(normed, up[:, part], preferred_element_type=jnp.float32)
             ).astype(jnp.bfloat16)
-            value = value + jnp.dot(hidden, down[part, :], preferred_element_type=jnp.float32)
+            product = jnp.dot(hidden, down[part, :], preferred_element_type=jnp.float32)
+            total = product if total is None else total + product
+        value = value + 0.5 * total
         return value.astype(jnp.bfloat16)
 
     def block_step(step, carry):
@@ -847,16 +863,14 @@
         conv_in[0:chunk, :] = value
         project(value, whole, gain_0, v0)
 
-        def attend_pair(piece, inner):
-            for fold in range(folds):
-                start = piece * (WIN * message) + fold * WIN
-                attend_window(
-                    [pl.ds(pl.multiple_of(start + r * message, WIN), WIN) for r in range(WIN)],
-                    block_bias,
-                )
-            return inner
-
-        lax.fori_loop(0, across, attend_pair, 0)
+        attend_windows(
+            [
+                [pl.ds(piece * (WIN * message) + fold * WIN + r * message, WIN) for r in range(WIN)]
+                for piece in range(across)
+                for fold in range(folds)
+            ],
+            block_bias,
+        )
         done = feed(conv_in[0:chunk, :], whole, gain_1, v1, v2, v3)
         section[pl.ds(step * batch, batch)] = done.reshape(batch, message, feats)
 
@@ -900,19 +914,21 @@
         for half in range(halves):
             project(rows_of(half), pl.ds(half * chunk, chunk), gain_2, v4)
 
-        def attend_pair(pair, inner):
-            for k in range(2):
-                attend_window(
+        def attend_some(step, inner):
+            attend_windows(
+                [
                     [
-                        pl.ds(r * columns * message + fold * WIN + 2 * pair + k, columns, stride=message)
+                        pl.ds(r * columns * message + fold * WIN + QUAD * step + k, columns, stride=message)
                         for r in range(rows_n)
                         for fold in range(folds)
-                    ],
-                    grid_bias,
-                )
+                    ]
+                    for k in range(QUAD)
+                ],
+                grid_bias,
+            )
             return inner
 
-        lax.fori_loop(0, part_rows // tokens // 2, attend_pair, 0)
+        lax.fori_loop(0, part_rows // tokens // QUAD, attend_some, 0)
 
         def feed_half(half, inner):
             rows = pl.ds(pl.multiple_of(half * chunk, chunk), chunk)
@@ -955,7 +971,8 @@
             ]
             for fold in range(folds):
                 line = jnp.concatenate([t[fold * WIN : (fold + 1) * WIN] for t in tiles], axis=0)
-                o_ref[fold * fold_rows + part * WIN + down] = line.astype(jnp.bfloat16)
+                start = (fold * fold_rows + part * WIN + down) * col_count
+                o_ref[pl.ds(pl.multiple_of(start, col_count), col_count), :] = line.astype(jnp.bfloat16)
             return inner
 
         return lax.fori_loop(0, WIN, put, carry)
@@ -992,7 +1009,7 @@
     dma = pltpu.SemaphoreType.DMA
     return pl.pallas_call(
         functools.partial(block_kernel, (parts, pieces, rows_n, columns), feats // heads_n),
-        out_shape=jax.ShapeDtypeStruct(latent.shape, half_type),
+        out_shape=jax.ShapeDtypeStruct((rows, feats), half_type),
         in_specs=[vmem] * 10 + [hbm] * 12,
         out_specs=vmem,
         scratch_shapes=[pltpu.VMEM(w.shape, half_type) for w in front]
@@ -1009,7 +1026,7 @@
             pltpu.VMEM((rows, feats), half_type),
             pltpu.VMEM((around, feats), half_type),
             pltpu.VMEM(
-                (width // LANES, (row_count + 2) * (col_count + PAD), LANES), jnp.float32
+                (width // LANES, PAD + (row_count + 2) * (col_count + PAD), LANES), jnp.float32
             ),
             pltpu.VMEM((parts * devices, message, width), half_type),
             pltpu.VMEM((8, width), jnp.float32),
@@ -1017,6 +1034,8 @@
             pltpu.VMEM((1, width), jnp.float32),
             pltpu.VMEM((heads_n, 4 * WIN * WIN), jnp.float32),
             bias, bias,
+            pltpu.VMEM((QUAD * heads_n // 8, 4 * WIN * WIN, 2 * WIN * WIN), jnp.float32),
+            pltpu.VMEM((QUAD * heads_n // 8, 4 * WIN * WIN, 2 * WIN * WIN), half_type),
             dma((12,)), dma((2, parts)), dma((2, parts)), dma((8,)), dma((8,)), dma, dma,
         ],
         compiler_params=pltpu.CompilerParams(
@@ -1025,7 +1044,7 @@
         name="whole_block",
     )(
         latent, scale[None], shift[None], taps, *tables, *[g[None] for g in gains], *front, *weights
-    )
+    ).reshape(latent.shape)
 
 
 def compact(row_count, col_count):

time: 94.9 us -> 82.3 us (0.87)
  Pallas kernels: 92.5 us -> 79.9 us
    pallas_call x1, Pallas kernels: 92.5 us -> 79.9 us  [whole_block(): pl.pallas_call(functools.partial(block_kernel, (parts, pieces, rows_n, co...]
where the time goes in v3:
time: 82.3 us; the launch traced here: 82.2 us
  Pallas kernels  79.9 us (97%)
  local copies, waits for them, and re-layouts  2.3 us (3%)
    pallas_call x1, Pallas kernels, whole_block(): pl.pallas_call(functools.partial(block_kernel, (parts, pieces, rows_n, co...  79.9 us
    unnamed x1, local copies, waits for them, and re-layouts  2.3 us

profile of v3, /device:TPU:5, one launch (start us, length us, event | category | flops | bytes accessed | tf_op | source)
XLA Modules:
  0.0 82.2 jit_solution(8912215356680221151)
XLA Ops:
  0.0 79.9 %whole_block.1 = bf16[1024,512]{1,0:T(8,128)(2,1)} custom-call(bf16[32,32,512]{2,1,0:T(8,128)(2,1)} %latent.1, f32[1,512]{1,0:T(1,128)} %bitcast.8, f32[1,512]{1,0:T(1,128)} %bitcast.9, f32[9,2048]{1,0:T(8,128)} %taps_in.1, f32[16,225]{1,0:T(8,128)} %block_table.1, f32[16,225]{1,0:T(8,128)} %grid_table.1, f32[1,512]{1,0:T(1,128)} %bitcast.10, ...), custom_call_target="tpu_custom_call" | custom-call | tf_op jit(solution)/shard_map/whole_block/pallas_call | solution.py:1010
  79.9 2.3 %copy.24 = bf16[32,32,512]{2,1,0:T(8,128)(2,1)} copy(bf16[32,32,512]{2,1,0:T(8,128)(2,1)} %bitcast.7) | data formatting | bytes 2097152

commit v4 on v3

--- a/solution.py
+++ b/solution.py
@@ -490,7 +490,7 @@
     h0, h1, h2, h3, w0, w1, w2, w3, w4, w5, w6, w7, o_ref,
     u0, u1, u2, u3, triple, heads, v0, v1, v2, v3, v4, v5, v6, v7,
     section, got, output, back, edges, halo, corner, conv_in, halo_in, expanded, deep_ref,
-    sums, slots, excite_ref, padded, block_bias, grid_bias, score_ref, share_ref,
+    sums, slots, excite_ref, padded, block_bias, grid_bias, score_ref, share_ref, half_taps,
     weight_sem, send_sem, recv_sem, halo_send, halo_recv, sum_send, sum_recv,
 ):
     parts, pieces, rows_n, columns = shape
@@ -565,7 +565,7 @@
         conv_in[8 * group * col_count : 8 * (group + 1) * col_count, :] = (
             cells.astype(jnp.float32) * scale_in[...] + shift_in[...]
         ).astype(jnp.bfloat16)
-    pl.semaphore_wait(barrier, devices - 1)
+    half_taps[...] = 0.5 * taps_in[...]
 
     def outgoing(k):
         if k < 4:
@@ -585,13 +585,6 @@
             device_id={"row": row_at + down, "col": col_at + side}, device_id_type=mesh_ids,
         )
 
-    ways = sides + CORNERS
-    for k, way in enumerate(ways):
-
-        @pl.when(near[way])
-        def _(k=k):
-            outgoing(k).start()
-
     moves[0].wait()
     block = 256
 
@@ -602,7 +595,7 @@
                 conv_in[8 * group * col_count : 8 * (group + 1) * col_count, :], u0[:, lanes],
                 preferred_element_type=jnp.float32,
             )
-            value = twice_gelu(product).astype(jnp.bfloat16).astype(jnp.float32)
+            value = twice_gelu(product.astype(jnp.bfloat16)).astype(jnp.float32)
             for r in range(8):
                 start = PAD + (1 + 8 * group + r) * wide
                 for half in range(block // LANES):
@@ -611,7 +604,16 @@
                     ]
         return carry
 
-    lax.fori_loop(0, width // block, expand, 0)
+    lax.fori_loop(0, width // block // 2, expand, 0)
+    pl.semaphore_wait(barrier, devices - 1)
+    ways = sides + CORNERS
+    for k, way in enumerate(ways):
+
+        @pl.when(near[way])
+        def _(k=k):
+            outgoing(k).start()
+
+    lax.fori_loop(width // block // 2, width // block, expand, 0)
     for k, way in enumerate(ways):
         opposite = (-way[0], -way[1])
         src_k = ways.index(opposite)
@@ -642,7 +644,7 @@
     def expand_halo(step, carry):
         lanes = pl.ds(pl.multiple_of(step * block, block), block)
         product = jnp.dot(halo_in[...], u0[:, lanes], preferred_element_type=jnp.float32)
-        value = twice_gelu(product).astype(jnp.bfloat16).astype(jnp.float32)
+        value = twice_gelu(product.astype(jnp.bfloat16)).astype(jnp.float32)
         up = jnp.where(near[(-1, 0)], value[:col_count], 0.0)
         low = jnp.where(near[(1, 0)], value[col_count : 2 * col_count], 0.0)
         left = jnp.where(near[(0, -1)], value[2 * col_count : 2 * col_count + row_count], 0.0)
@@ -666,7 +668,7 @@
 
     def depth(step, carry):
         lanes = pl.ds(pl.multiple_of(step * LANES, LANES), LANES)
-        taps = [0.5 * taps_in[k : k + 1, lanes] for k in range(9)]
+        taps = [half_taps[k : k + 1, lanes] for k in range(9)]
 
         def pair_of_rows(group, total):
             results = []
@@ -701,7 +703,7 @@
             return total
 
         sums[:, lanes] = lax.fori_loop(
-            0, fold_rows // 2, pair_of_rows, jnp.zeros((8, LANES), jnp.float32)
+            0, fold_rows // 2, pair_of_rows, jnp.zeros((8, LANES), jnp.float32), unroll=2
         )
         return carry
 
@@ -831,8 +833,8 @@
         for k in range(up.shape[1] // tile):
             part = slice(k * tile, (k + 1) * tile)
             hidden = twice_gelu(
-                jnp.dot(normed, up[:, part], preferred_element_type=jnp.float32)
-            ).astype(jnp.bfloat16)
+                jnp.dot(normed, up[:, part], preferred_element_type=jnp.float32).astype(jnp.bfloat16)
+            )
             product = jnp.dot(hidden, down[part, :], preferred_element_type=jnp.float32)
             total = product if total is None else total + product
         value = value + 0.5 * total
@@ -1036,10 +1038,11 @@
             bias, bias,
             pltpu.VMEM((QUAD * heads_n // 8, 4 * WIN * WIN, 2 * WIN * WIN), jnp.float32),
             pltpu.VMEM((QUAD * heads_n // 8, 4 * WIN * WIN, 2 * WIN * WIN), half_type),
+            pltpu.VMEM(taps.shape, jnp.float32),
             dma((12,)), dma((2, parts)), dma((2, parts)), dma((8,)), dma((8,)), dma, dma,
         ],
         compiler_params=pltpu.CompilerParams(
-            collective_id=3, has_side_effects=True, vmem_limit_bytes=60 * 1024 * 1024
+            collective_id=3, has_side_effects=True, vmem_limit_bytes=50 * 1024 * 1024
         ),
         name="whole_block",
     )(

time: 82.3 us -> 90.2 us (1.096)
  local copies, waits for them, and re-layouts: 2.3 us -> 11.6 us
  Pallas kernels: 79.9 us -> 78 us
    unnamed x1 -> x27, local copies, waits for them, and re-layouts: 2.3 us -> 11.6 us
    pallas_call x1, Pallas kernels: 79.9 us -> 78 us  [whole_block(): pl.pallas_call(functools.partial(block_kernel, (parts, pieces, rows_n, co...]
where the time goes in v4:
time: 90.2 us; the launch traced here: 89.6 us
  Pallas kernels  78 us (86%)
  local copies, waits for them, and re-layouts  11.6 us (13%)
    pallas_call x1, Pallas kernels, whole_block(): pl.pallas_call(functools.partial(block_kernel, (parts, pieces, rows_n, co...  78 us
    unnamed x27, local copies, waits for them, and re-layouts  11.6 us

profile of v4, /device:TPU:5, one launch (start us, length us, event | category | flops | bytes accessed | tf_op | source)
XLA Modules:
  0.0 89.6 jit_solution(5640670434351651965)
XLA Ops:
  0.0 0.0 copy-start
  0.0 1.0 %copy-done = bf16[2048,128]{1,0:T(8,128)(2,1)S(1)} copy-done((bf16[2048,128]{1,0:T(8,128)(2,1)S(1)}, bf16[2048,128]{1,0:T(8,128)(2,1)}, u32[]{:S(2)}) %copy-start) | copy-done | bytes 524312
  1.0 0.0 copy-start.1
  1.0 1.0 %copy-done.1 = bf16[128,2048]{1,0:T(8,128)(2,1)S(1)} copy-done((bf16[128,2048]{1,0:T(8,128)(2,1)S(1)}, bf16[128,2048]{1,0:T(8,128)(2,1)}, u32[]{:S(2)}) %copy-start.1) | copy-done | bytes 524312
  2.1 0.0 copy-start.2
  2.1 1.0 %copy-done.2 = bf16[512,512]{1,0:T(8,128)(2,1)S(1)} copy-done((bf16[512,512]{1,0:T(8,128)(2,1)S(1)}, bf16[512,512]{1,0:T(8,128)(2,1)}, u32[]{:S(2)}) %copy-start.2) | copy-done | bytes 524312
  3.1 0.0 copy-start.3
  3.1 1.0 %copy-done.3 = bf16[512,512]{1,0:T(8,128)(2,1)S(1)} copy-done((bf16[512,512]{1,0:T(8,128)(2,1)S(1)}, bf16[512,512]{1,0:T(8,128)(2,1)}, u32[]{:S(2)}) %copy-start.3) | copy-done | bytes 524312
  4.2 0.0 copy-start.4
  4.2 0.9 %copy-done.4 = f32[9,2048]{1,0:T(8,128)S(1)} copy-done((f32[9,2048]{1,0:T(8,128)S(1)}, f32[9,2048]{1,0:T(8,128)}, u32[]{:S(2)}) %copy-start.4) | copy-done | bytes 73752
  5.1 0.0 copy-start.5
  5.1 0.7 copy-done.5
  5.8 0.0 copy-start.6
  5.8 0.7 copy-done.6
  6.5 0.0 copy-start.7
  6.5 0.7 copy-done.7
  7.2 0.0 copy-start.8
  7.2 0.7 copy-done.8
  7.9 0.0 copy-start.9
  7.9 0.7 copy-done.9
  8.6 0.0 copy-start.10
  8.6 0.7 copy-done.10
  9.2 0.0 copy-start.11
  9.2 0.7 copy-done.11
  9.9 0.0 copy-start.12
  9.9 0.7 copy-done.12
  10.6 78.0 %whole_block.1 = bf16[1024,512]{1,0:T(8,128)(2,1)S(1)} custom-call(bf16[32,32,512]{2,1,0:T(8,128)(2,1)} %latent.1, f32[1,512]{1,0:T(1,128)S(1)} %bitcast.8, f32[1,512]{1,0:T(1,128)S(1)} %bitcast.9, f32[9,2048]{1,0:T(8,128)S(1)} %copy-done.4, f32[16,225]{1,0:T(8,128)S(1)} %copy-done.5, f32[16,225]{1,0:T(8,128)S(1)} %copy-done.6, f32[1,512]{1,0:T(1,128)S(1)} %bitcast.10, ...), custom_call_target="tpu_custom_call" | custom-call | tf_op jit(solution)/shard_map/whole_block/pallas_call | solution.py:1012
  88.6 1.0 %copy.24 = bf16[32,32,512]{2,1,0:T(8,128)(2,1)} copy(bf16[32,32,512]{2,1,0:T(8,128)(2,1)S(1)} %bitcast.7) | data formatting | bytes 2097152
Async XLA Ops:
  0.0 1.0 %copy-start = (bf16[2048,128]{1,0:T(8,128)(2,1)S(1)}, bf16[2048,128]{1,0:T(8,128)(2,1)}, u32[]{:S(2)}) copy-start(bf16[2048,128]{1,0:T(8,128)(2,1)} %h1.1) | copy-start | bytes 1572868
  1.0 1.0 %copy-start.1 = (bf16[128,2048]{1,0:T(8,128)(2,1)S(1)}, bf16[128,2048]{1,0:T(8,128)(2,1)}, u32[]{:S(2)}) copy-start(bf16[128,2048]{1,0:T(8,128)(2,1)} %h2.1) | copy-start | bytes 1572868
  2.1 1.0 %copy-start.2 = (bf16[512,512]{1,0:T(8,128)(2,1)S(1)}, bf16[512,512]{1,0:T(8,128)(2,1)}, u32[]{:S(2)}) copy-start(bf16[512,512]{1,0:T(8,128)(2,1)} %w1.1) | copy-start | bytes 1572868
  3.1 1.0 %copy-start.3 = (bf16[512,512]{1,0:T(8,128)(2,1)S(1)}, bf16[512,512]{1,0:T(8,128)(2,1)}, u32[]{:S(2)}) copy-start(bf16[512,512]{1,0:T(8,128)(2,1)} %w5.1) | copy-start | bytes 1572868
  4.2 0.9 %copy-start.4 = (f32[9,2048]{1,0:T(8,128)S(1)}, f32[9,2048]{1,0:T(8,128)}, u32[]{:S(2)}) copy-start(f32[9,2048]{1,0:T(8,128)} %taps_in.1) | copy-start | bytes 221188
  5.1 0.7 copy-start.5
  5.8 0.7 copy-start.6
  6.5 0.7 copy-start.7
  7.2 0.7 copy-start.8
  7.9 0.7 copy-start.9
  8.6 0.7 copy-start.10
  9.2 0.7 copy-start.11
  9.9 0.7 copy-start.12

commit v5 on v4

--- a/solution.py
+++ b/solution.py
@@ -485,7 +485,7 @@
 
 
 def block_kernel(
-    shape, head_size, latent, scale_in, shift_in, taps_in, block_table, grid_table,
+    shape, head_size, ready, latent, scale_in, shift_in, taps_in, block_table, grid_table,
     gain_0, gain_1, gain_2, gain_3,
     h0, h1, h2, h3, w0, w1, w2, w3, w4, w5, w6, w7, o_ref,
     u0, u1, u2, u3, triple, heads, v0, v1, v2, v3, v4, v5, v6, v7,
@@ -532,6 +532,7 @@
     ]
     for move in moves:
         move.start()
+    ready()
 
     near = {
         (down, side): jnp.logical_and(
@@ -668,38 +669,39 @@
 
     def depth(step, carry):
         lanes = pl.ds(pl.multiple_of(step * LANES, LANES), LANES)
-        taps = [half_taps[k : k + 1, lanes] for k in range(9)]
+        taps = [half_taps[k : k + 1, lanes].astype(jnp.bfloat16) for k in range(9)]
 
         def pair_of_rows(group, total):
-            results = []
-            for fold in range(folds):
-                first = fold * fold_rows + 2 * group
-                base = pl.multiple_of(first * wide, 8)
-                held = [
+            def cells(k, side):
+                lines = []
+                for fold in range(folds):
+                    base = pl.multiple_of((fold * fold_rows + 2 * group) * wide, 8)
+                    lines.append(expanded[step, pl.ds(base + (PAD + k * wide + side), col_count), :])
+                return jnp.concatenate(
                     [
-                        expanded[step, pl.ds(base + (PAD + k * wide + side), col_count), :]
-                        for side in (-1, 0, 1)
-                    ]
-                    for k in range(4)
-                ]
-                for k in range(2):
-                    summed = sum(
-                        held[k + down][side] * taps[3 * down + side]
-                        for down in range(3)
-                        for side in range(3)
-                    )
-                    value = twice_gelu(summed)
-                    total = total + jnp.sum(value.reshape(col_count // 8, 8, LANES), axis=0)
-                    results.append(value)
+                        line[piece * WIN : (piece + 1) * WIN]
+                        for piece in range(pieces)
+                        for line in lines
+                    ],
+                    axis=0,
+                ).astype(jnp.bfloat16)
+
+            held = [[cells(k, side) for side in (-1, 0, 1)] for k in range(4)]
             part, down = lax.div(2 * group, WIN), lax.rem(2 * group, WIN)
             for k in range(2):
+                columns_of = [
+                    held[k][side] * taps[side]
+                    + held[k + 1][side] * taps[3 + side]
+                    + held[k + 2][side] * taps[6 + side]
+                    for side in range(3)
+                ]
+                value = twice_gelu(columns_of[0] + columns_of[2] + columns_of[1])
+                total = total + jnp.sum(
+                    value.astype(jnp.float32).reshape(-1, 8, LANES), axis=0
+                )
                 for piece in range(pieces):
-                    rows = slice(piece * WIN, (piece + 1) * WIN)
-                    tile = jnp.concatenate(
-                        [results[2 * fold + k][rows] for fold in range(folds)], axis=0
-                    )
                     at = part * devices + piece * WIN + down + k
-                    deep_ref[at, :, lanes] = tile.astype(jnp.bfloat16)
+                    deep_ref[at, :, lanes] = value[piece * message : (piece + 1) * message]
             return total
 
         sums[:, lanes] = lax.fori_loop(
@@ -993,6 +995,21 @@
             pltpu.make_async_copy(target, target, halo_send.at[k]).wait()
 
 
+def fetch_and_run(shape, head_size, count, latent, *refs):
+    smalls, refs, held, sem = refs[:count], refs[count : -count - 1], refs[-count - 1 : -1], refs[-1]
+    copies = [
+        pltpu.make_async_copy(src, dst, sem.at[k]) for k, (src, dst) in enumerate(zip(smalls, held))
+    ]
+    for copy in copies:
+        copy.start()
+
+    def ready():
+        for copy in copies:
+            copy.wait()
+
+    block_kernel(shape, head_size, ready, latent, *held, *refs)
+
+
 def whole_block(latent, scale, shift, taps, tables, gains, front, weights):
     row_count, col_count, feats = latent.shape
     rows_n, columns = lax.axis_size("row"), lax.axis_size("col")
@@ -1009,10 +1026,13 @@
     mail = pltpu.VMEM((parts * devices, message, feats), half_type)
     bias = pltpu.VMEM((heads_n // 8, 4 * WIN * WIN, 2 * WIN * WIN), jnp.float32)
     dma = pltpu.SemaphoreType.DMA
+    smalls = (scale[None], shift[None], taps, *tables, *[g[None] for g in gains])
     return pl.pallas_call(
-        functools.partial(block_kernel, (parts, pieces, rows_n, columns), feats // heads_n),
+        functools.partial(
+            fetch_and_run, (parts, pieces, rows_n, columns), feats // heads_n, len(smalls)
+        ),
         out_shape=jax.ShapeDtypeStruct((rows, feats), half_type),
-        in_specs=[vmem] * 10 + [hbm] * 12,
+        in_specs=[vmem] + [hbm] * (len(smalls) + 12),
         out_specs=vmem,
         scratch_shapes=[pltpu.VMEM(w.shape, half_type) for w in front]
         + [
@@ -1040,13 +1060,15 @@
             pltpu.VMEM((QUAD * heads_n // 8, 4 * WIN * WIN, 2 * WIN * WIN), half_type),
             pltpu.VMEM(taps.shape, jnp.float32),
             dma((12,)), dma((2, parts)), dma((2, parts)), dma((8,)), dma((8,)), dma, dma,
-        ],
+        ]
+        + [pltpu.VMEM(small.shape, jnp.float32) for small in smalls]
+        + [dma((len(smalls),))],
         compiler_params=pltpu.CompilerParams(
-            collective_id=3, has_side_effects=True, vmem_limit_bytes=50 * 1024 * 1024
+            collective_id=3, has_side_effects=True, vmem_limit_bytes=54 * 1024 * 1024
         ),
         name="whole_block",
     )(
-        latent, scale[None], shift[None], taps, *tables, *[g[None] for g in gains], *front, *weights
+        latent, *smalls, *front, *weights
     ).reshape(latent.shape)
 
 

time: 90.2 us -> 79.7 us (0.88)
  local copies, waits for them, and re-layouts: 11.6 us -> 2.3 us
    unnamed x27 -> x1, local copies, waits for them, and re-layouts: 11.6 us -> 2.3 us
where the time goes in v5:
time: 79.7 us; the launch traced here: 79.5 us
  Pallas kernels  77.2 us (97%)
  local copies, waits for them, and re-layouts  2.3 us (3%)
    pallas_call x1, Pallas kernels, whole_block(): pl.pallas_call(functools.partial(fetch_and_run, (parts, pieces, rows_n, c...  77.2 us
    unnamed x1, local copies, waits for them, and re-layouts  2.3 us

profile of v5, /device:TPU:5, one launch (start us, length us, event | category | flops | bytes accessed | tf_op | source)
XLA Modules:
  0.0 79.5 jit_solution(1494311096985317870)
XLA Ops:
  0.0 77.2 %whole_block.1 = bf16[1024,512]{1,0:T(8,128)(2,1)} custom-call(bf16[32,32,512]{2,1,0:T(8,128)(2,1)} %latent.1, f32[1,512]{1,0:T(1,128)} %bitcast.8, f32[1,512]{1,0:T(1,128)} %bitcast.9, f32[9,2048]{1,0:T(8,128)} %refs_2_.1, f32[16,225]{1,0:T(8,128)} %refs_3_.1, f32[16,225]{1,0:T(8,128)} %refs_4_.1, f32[1,512]{1,0:T(1,128)} %bitcast.10, f32[1,512]{1,0:T(1,128)} %bitcast.11, ...), custom_call_target="tpu_custom_call" | custom-call | tf_op jit(solution)/shard_map/whole_block/pallas_call | solution.py:1030
  77.2 2.3 %copy.24 = bf16[32,32,512]{2,1,0:T(8,128)(2,1)} copy(bf16[32,32,512]{2,1,0:T(8,128)(2,1)} %bitcast.7) | data formatting | bytes 2097152
